TPU v7x, 512 devices: a whole 4x4x16 slice. The times are simulated.
512 devices in a mesh: gx: 32 (over x, z_hi, core), gy: 16 (over y, z_lo).
Axes of the slice: x: 4, y: 4, z: 16 (z_hi: 4, z_lo: 4; z = z_hi * 4 + z_lo), core: 2. Of those that a mesh axis runs over, the one named last changes fastest.
Arguments:
- populations: float32 [19, 256, 256, 128], P(None, 'gx', 'gy'), may hold values from 0.02 to 0.1
- solid: int32 [256, 256, 128], P('gx', 'gy'), may hold values 0 or 1
- visible: int32 [16, 16, 8], replicated, may hold values 0 or 1
- omega: float32 [1], replicated, may hold values from 1 to 1.6
- iso_levels: float32 [8], replicated, may hold values from -1 to 1
- iso_index: int32 [16, 16], replicated, may hold values from 0 to 7
Outputs:
- new_populations: float32 [19, 256, 256, 128], P(None, 'gx', 'gy')
- q_field: float32 [256, 256, 128], P('gx', 'gy')
- crossings: float32 [3, 256, 256, 128], P(None, 'gx', 'gy')
All inputs are finite; a program needn't handle non-finite values. No bound on the sum of `solid` on one device may be relied on, other than what follows from the above.
Results may differ from a plain program's by a relative error of at most 0.000033.
Values sent between devices are 32-bit elements; how exact they have to be, the bound alone decides.
No kernel may reach another device: no remote copies, remote signals or barrier semaphores. Data moves between devices by JAX's collectives and lax.ppermute only.
A program may use at most 64 MiB of HBM per device.

v0:
```python
import jax
import jax.numpy as jnp
from jax import lax
from jax.sharding import PartitionSpec as P

BRICK = 16
LEVELS = 8


LATTICE = [
    (0, 0, 0),
    (1, 0, 0),
    (-1, 0, 0),
    (0, 1, 0),
    (0, -1, 0),
    (0, 0, 1),
    (0, 0, -1),
    (1, 1, 0),
    (-1, -1, 0),
    (1, -1, 0),
    (-1, 1, 0),
    (1, 0, 1),
    (-1, 0, -1),
    (1, 0, -1),
    (-1, 0, 1),
    (0, 1, 1),
    (0, -1, -1),
    (0, 1, -1),
    (0, -1, 1),
]
OPPOSITE = [0, 2, 1, 4, 3, 6, 5, 8, 7, 10, 9, 12, 11, 14, 13, 16, 15, 18, 17]
WEIGHTS = [1.0 / 3.0] + [1.0 / 18.0] * 6 + [1.0 / 36.0] * 12


def padded_2(shard, sides, width):
    for axis, dim in sides:
        size, length = (lax.axis_size(axis), shard.shape[dim])
        up = [(i, (i + 1) % size) for i in range(size)]
        down = [(j, i) for i, j in up]
        last = lax.slice_in_dim(shard, length - width, length, axis=dim)
        initial = lax.slice_in_dim(shard, 0, width, axis=dim)
        before = lax.ppermute(last, axis, up)
        after = lax.ppermute(initial, axis, down)
        shard = jnp.concatenate([before, shard, after], axis=dim)
    return shard


def moments(stacked):
    density = stacked[0]
    for number in range(1, 19):
        density = density + stacked[number]
    velocity = []
    for direction in range(3):
        total = jnp.zeros_like(density)
        for number in range(19):
            component = LATTICE[number][direction]
            if component == 1:
                total = total + stacked[number]
            elif component == -1:
                total = total - stacked[number]
        velocity.append(total / density)
    return (density, velocity)


def collide(populations, solid, rate):
    density, velocity = moments(populations)
    speed = velocity[0] * velocity[0] + velocity[1] * velocity[1] + velocity[2] * velocity[2]
    collided = []
    for number in range(19):
        projection = jnp.zeros_like(density)
        for direction in range(3):
            component = LATTICE[number][direction]
            if component == 1:
                projection = projection + velocity[direction]
            elif component == -1:
                projection = projection - velocity[direction]
        equilibrium = (
            WEIGHTS[number]
            * density
            * (1.0 + 3.0 * projection + 4.5 * projection * projection - 1.5 * speed)
        )
        relaxed = populations[number] - rate * (populations[number] - equilibrium)
        collided.append(jnp.where(solid == 1, populations[OPPOSITE[number]], relaxed))
    return collided


def crossing(here, there):
    return jnp.maximum(-here * there, 0.0) / (here * here + there * there + 0.25)


def expand_bricks(table, width_x, width_y):
    start_x = lax.axis_index("gx") * width_x
    start_y = lax.axis_index("gy") * width_y
    rows = lax.dynamic_slice_in_dim(table, start_x // BRICK, max(width_x // BRICK, 1), 0)
    rows = lax.dynamic_slice_in_dim(jnp.repeat(rows, BRICK, axis=0), start_x % BRICK, width_x, 0)
    rows = lax.dynamic_slice_in_dim(rows, start_y // BRICK, max(width_y // BRICK, 1), 1)
    return jnp.repeat(rows, BRICK, axis=1)


def per_device(populations, solid, visible, omega, iso_levels, iso_index):
    width_x = populations.shape[1]
    width_y = populations.shape[2]
    collided = collide(populations, solid, omega[0])
    padded = padded_2(jnp.stack(collided), (("gx", 1), ("gy", 2)), 1)
    read = []
    for number in range(19):
        step_x, step_y, step_z = LATTICE[number]
        plane = padded[number, 1 - step_x : 1 - step_x + width_x, 1 - step_y : 1 - step_y + width_y]
        read.append(jnp.roll(plane, step_z, axis=2))
    new_populations = jnp.stack(read)
    flow_density, flow = moments(read)
    rimmed = padded_2(jnp.stack(flow), (("gx", 1), ("gy", 2)), 3)

    def window(offset_x, offset_y):
        return rimmed[
            :, 3 + offset_x : 4 + offset_x + width_x, 3 + offset_y : 4 + offset_y + width_y, :
        ]

    along_x = (-window(2, 0) + 8.0 * window(1, 0) - 8.0 * window(-1, 0) + window(-2, 0)) / 12.0
    along_y = (-window(0, 2) + 8.0 * window(0, 1) - 8.0 * window(0, -1) + window(0, -2)) / 12.0
    centre = window(0, 0)
    along_z = (
        -jnp.roll(centre, -2, 3)
        + 8.0 * jnp.roll(centre, -1, 3)
        - 8.0 * jnp.roll(centre, 1, 3)
        + jnp.roll(centre, 2, 3)
    ) / 12.0
    grads = [[along_x[first], along_y[first], along_z[first]] for first in range(3)]
    inner = grads[0][0] * grads[0][0] + grads[1][1] * grads[1][1] + grads[2][2] * grads[2][2]
    inner = inner + 2.0 * (
        grads[0][1] * grads[1][0] + grads[0][2] * grads[2][0] + grads[1][2] * grads[2][1]
    )
    scaled = -50.0 * inner
    choose = iso_index[:, :, None] == jnp.arange(LEVELS, dtype=jnp.int32)[None, None, :]
    brick_levels = jnp.sum(jnp.where(choose, iso_levels[None, None, :], 0.0), axis=2)
    level = expand_bricks(brick_levels, width_x, width_y)[:, :, None]
    inside = scaled[:width_x, :width_y]
    here = inside - level
    shown = jnp.repeat(expand_bricks(visible, width_x, width_y), BRICK, axis=2) == 1
    weight_x = crossing(here, scaled[1 : width_x + 1, :width_y] - level)
    weight_y = crossing(here, scaled[:width_x, 1 : width_y + 1] - level)
    weight_z = crossing(here, jnp.roll(inside, -1, 2) - level)
    weights = jnp.stack(
        [
            jnp.where(shown, weight_x, 0.0),
            jnp.where(shown, weight_y, 0.0),
            jnp.where(shown, weight_z, 0.0),
        ]
    )
    q_field = jnp.where(shown, inside, 0.0)
    return (new_populations, q_field, weights)


def solution(mesh):
    in_specs = (P(None, "gx", "gy", None), P("gx", "gy", None), P(), P(), P(), P())
    out_specs = (P(None, "gx", "gy", None), P("gx", "gy", None), P(None, "gx", "gy", None))
    return jax.shard_map(
        per_device, mesh=mesh, in_specs=in_specs, out_specs=out_specs, check_vma=False
    )
```

profile of v0, /device:TPU:16, one launch (start us, length us, event | category | flops | bytes accessed | tf_op | source)
XLA Modules:
  0.0 82.7 jit_solution(4456389066203332384)
XLA Ops:
  1.3 1.5 %constant_dynamic-update-slice_fusion.37 = (f32[19,8,16,128]{3,2,1,0:T(8,128)S(1)}, f32[8,16,128]{2,1,0:T(8,128)S(1)}, f32[8,16,128]{2,1,0:T(8,128)S(1)}, f32[8,...) fusion(f32[]{:T(128)} %bitcast.505, ...), kind=kLoop, calls=%fused_computation.102 | loop fusion | flops 1015807 | bytes 1785860
  2.8 0.0 copy-start
  2.8 0.1 copy.27
  2.9 1.2 %copy-done = f32[19,8,16,128]{3,2,1,0:T(8,128)S(1)} copy-done((f32[19,8,16,128]{3,2,1,0:T(8,128)S(1)}, f32[19,8,16,128]{3,2,1,0:T(8,128)}, u32[]{:S(2)}) %copy-start) | copy-done | bytes 1245208
  4.8 0.0 copy-start.2
  4.8 0.0 copy-start.3
  5.0 14.4 %collective-permute-start.1 = (f32[19,1,16,128]{3,2,1,0:T(8,128)S(1)}, f32[19,1,16,128]{3,2,1,0:T(8,128)S(1)}, u32[]{:S(2)}, u32[]{:S(2)}) collective-permute-start(f32[19,1,16,128]{3,2,1,0:T(8,128)S(1)} %get-tuple-element.48), channel_id=1, source_target_pairs={{16,0},{32,16},{48,32},{64,48},{80,64},{96,80},{112,96},{128,112},... | collective-permute-start | bytes 466952 | tf_op jit(solution)/shard_map/ppermute | solution.py:43
  19.4 1.9 %collective-permute-start = (f32[19,1,16,128]{3,2,1,0:T(8,128)S(1)}, f32[19,1,16,128]{3,2,1,0:T(8,128)S(1)}, u32[]{:S(2)}, u32[]{:S(2)}) collective-permute-start(f32[19,1,16,128]{3,2,1,0:T(8,128)S(1)} %get-tuple-element.47), channel_id=1, source_target_pairs={{0,16},{16,32},{32,48},{48,64},{64,80},{80,96},{96,112},{112,128},... | collective-permute-start | bytes 466952 | tf_op jit(solution)/shard_map/ppermute | solution.py:42
  21.3 0.1 slice.511
  21.4 0.1 slice.509
  21.5 0.0 copy-done.2
  21.5 0.0 copy-done.3
  21.5 0.1 select_reduce_fusion
  21.6 0.6 dynamic_slice.5
  22.2 0.9 %fusion.200 = pred[8]{0:T(512)(128)(4,1)S(1)} fusion(s32[16,16,8]{1,2,0:T(8,128)} %param.8, s32[]{:T(128)S(6)} %select_n.126, s32[]{:T(128)S(6)} %select_n.129), kind=kLoop, calls=%fused_computation.389 | loop fusion | flops 8 | bytes 48 | tf_op jit(solution)/shard_map/eq | solution.py:139
  23.1 0.1 broadcast_in_dim.31
  23.1 0.1 eq.23
  23.2 3.9 %collective-permute-done.1 = f32[19,1,16,128]{3,2,1,0:T(8,128)S(1)} collective-permute-done((f32[19,1,16,128]{3,2,1,0:T(8,128)S(1)}, f32[19,1,16,128]{3,2,1,0:T(8,128)S(1)}, u32[]{:S(2)}, u32[]{:S(2)}) %collective-permute-start.1) | collective-permute-done | bytes 155680 | tf_op jit(solution)/shard_map/ppermute | solution.py:43
  27.1 9.4 %collective-permute-done = f32[19,1,16,128]{3,2,1,0:T(8,128)S(1)} collective-permute-done((f32[19,1,16,128]{3,2,1,0:T(8,128)S(1)}, f32[19,1,16,128]{3,2,1,0:T(8,128)S(1)}, u32[]{:S(2)}, u32[]{:S(2)}) %collective-permute-start) | collective-permute-done | bytes 155680 | tf_op jit(solution)/shard_map/ppermute | solution.py:42
  36.5 0.1 pad_maximum_fusion.4
  36.6 1.9 %collective-permute-start.2 = (f32[19,10,1,128]{3,2,1,0:T(1,128)S(1)}, f32[19,10,1,128]{3,2,1,0:T(1,128)S(1)}, u32[]{:S(2)}, u32[]{:S(2)}) collective-permute-start(f32[19,10,1,128]{3,2,1,0:T(1,128)S(1)} %get-tuple-element.39), channel_id=1, source_target_pairs={{0,1},{1,2},{2,3},{3,4},{4,5},{5,6},{6,7},{7,8},{8,9},{9,10},{10,1... | collective-permute-start | bytes 291848 | tf_op jit(solution)/shard_map/ppermute | solution.py:42
  38.5 6.6 %collective-permute-start.3 = (f32[19,10,1,128]{3,2,1,0:T(1,128)S(1)}, f32[19,10,1,128]{3,2,1,0:T(1,128)S(1)}, u32[]{:S(2)}, u32[]{:S(2)}) collective-permute-start(f32[19,10,1,128]{3,2,1,0:T(1,128)S(1)} %get-tuple-element.40), channel_id=1, source_target_pairs={{1,0},{2,1},{3,2},{4,3},{5,4},{6,5},{7,6},{8,7},{9,8},{10,9},{11,1... | collective-permute-start | bytes 291848 | tf_op jit(solution)/shard_map/ppermute | solution.py:43
  45.2 0.1 slice.519
  45.3 0.1 slice.517
  45.4 0.1 slice.515
  45.4 0.1 slice.513
  45.5 2.6 %collective-permute-done.2 = f32[19,10,1,128]{3,2,1,0:T(1,128)S(1)} collective-permute-done((f32[19,10,1,128]{3,2,1,0:T(1,128)S(1)}, f32[19,10,1,128]{3,2,1,0:T(1,128)S(1)}, u32[]{:S(2)}, u32[]{:S(2)}) %collective-permute-start.2) | collective-permute-done | bytes 97312 | tf_op jit(solution)/shard_map/ppermute | solution.py:42
  48.2 0.0 collective-permute-done.3
  48.2 0.1 slice.527
  48.3 0.1 slice.525
  48.4 0.1 slice.523
  48.5 0.1 slice.521
  48.6 0.3 fusion.192
  48.9 0.1 constant_dynamic-update-slice_fusion.32
  49.0 0.1 constant_dynamic-update-slice_fusion.31
  49.3 0.1 fusion.197
  49.4 1.9 %collective-permute-start.5 = (f32[3,3,16,128]{3,2,1,0:T(8,128)S(1)}, f32[3,3,16,128]{3,2,1,0:T(8,128)S(1)}, u32[]{:S(2)}, u32[]{:S(2)}) collective-permute-start(f32[3,3,16,128]{3,2,1,0:T(8,128)S(1)} %get-tuple-element.66), channel_id=1, source_target_pairs={{16,0},{32,16},{48,32},{64,48},{80,64},{96,80},{112,96},{128,112},... | collective-permute-start | bytes 221192 | tf_op jit(solution)/shard_map/ppermute | solution.py:43
  51.4 2.4 %collective-permute-start.4 = (f32[3,3,16,128]{3,2,1,0:T(8,128)S(1)}, f32[3,3,16,128]{3,2,1,0:T(8,128)S(1)}, u32[]{:S(2)}, u32[]{:S(2)}) collective-permute-start(f32[3,3,16,128]{3,2,1,0:T(8,128)S(1)} %get-tuple-element.65), channel_id=1, source_target_pairs={{0,16},{16,32},{32,48},{48,64},{64,80},{80,96},{96,112},{112,128},... | collective-permute-start | bytes 221192 | tf_op jit(solution)/shard_map/ppermute | solution.py:42
  53.8 0.0 collective-permute-done.5
  53.8 9.3 %collective-permute-done.4 = f32[3,3,16,128]{3,2,1,0:T(8,128)S(1)} collective-permute-done((f32[3,3,16,128]{3,2,1,0:T(8,128)S(1)}, f32[3,3,16,128]{3,2,1,0:T(8,128)S(1)}, u32[]{:S(2)}, u32[]{:S(2)}) %collective-permute-start.4) | collective-permute-done | bytes 73760 | tf_op jit(solution)/shard_map/ppermute | solution.py:42
  63.1 6.8 %collective-permute-start.6 = (f32[3,14,3,128]{3,2,1,0:T(4,128)S(1)}, f32[3,14,3,128]{3,2,1,0:T(4,128)S(1)}, u32[]{:S(2)}, u32[]{:S(2)}) collective-permute-start(f32[3,14,3,128]{3,2,1,0:T(4,128)S(1)} %get-tuple-element.61), channel_id=1, source_target_pairs={{1,0},{2,1},{3,2},{4,3},{5,4},{6,5},{7,6},{8,7},{9,8},{10,9},{11,1... | collective-permute-start | bytes 193544 | tf_op jit(solution)/shard_map/ppermute | solution.py:43
  70.0 1.9 %collective-permute-start.7 = (f32[3,14,3,128]{3,2,1,0:T(4,128)S(1)}, f32[3,14,3,128]{3,2,1,0:T(4,128)S(1)}, u32[]{:S(2)}, u32[]{:S(2)}) collective-permute-start(f32[3,14,3,128]{3,2,1,0:T(4,128)S(1)} %get-tuple-element.62), channel_id=1, source_target_pairs={{0,1},{1,2},{2,3},{3,4},{4,5},{5,6},{6,7},{7,8},{8,9},{9,10},{10,1... | collective-permute-start | bytes 193544 | tf_op jit(solution)/shard_map/ppermute | solution.py:42
  71.9 0.0 copy-start.1
  72.0 0.1 collective-permute-done.6
  72.1 7.0 %collective-permute-done.7 = f32[3,14,3,128]{3,2,1,0:T(4,128)S(1)} collective-permute-done((f32[3,14,3,128]{3,2,1,0:T(4,128)S(1)}, f32[3,14,3,128]{3,2,1,0:T(4,128)S(1)}, u32[]{:S(2)}, u32[]{:S(2)}) %collective-permute-start.7) | collective-permute-done | bytes 64544 | tf_op jit(solution)/shard_map/ppermute | solution.py:42
  79.1 0.1 pad_maximum_fusion
  79.2 0.2 fusion.209
  79.3 0.0 copy-done.1
  79.3 0.2 fusion.208
  79.5 0.2 fusion.211
  79.7 0.2 fusion.210
  79.8 0.6 fusion.3
  80.5 0.1 fusion.14
  80.6 0.1 slice.557
  80.6 1.3 %select_bitcast_fusion.2 = (f32[1,8,16,128]{3,2,1,0:T(8,128)S(1)}, f32[1,8,16,128]{3,2,1,0:T(8,128)S(1)}, f32[1,8,16,128]{3,2,1,0:T(8,128)S(1)}, f32[8,16,128]{2,1,0:T(8,128)}) fusion(f32[9,17,128]{2,1,0:T(8,128)S(1)} %fusion.14, f32[]{:T(128)} %bitcast.69, pred[128]{0:T(512)(128)(4,1)S(1)} %eq.23, f32[8,16,1]{2,1,0:T(8,128)S(1)} %slice.558, ...), kind=kLoop, calls=%fused_computation.376 | loop fusion | flops 475136 | bytes 524420 | tf_op jit(solution)/shard_map/stack | solution.py:143
  82.0 0.7 pad_maximum_fusion.1
  (40 shorter events, 1.0 us)
Async XLA Ops:
  2.8 1.3 %copy-start = (f32[19,8,16,128]{3,2,1,0:T(8,128)S(1)}, f32[19,8,16,128]{3,2,1,0:T(8,128)}, u32[]{:S(2)}) copy-start(f32[19,8,16,128]{3,2,1,0:T(8,128)} %param.6) | copy-start | bytes 3735556
  4.8 16.7 %copy-start.2 = (s32[16,16]{1,0:T(8,128)S(1)}, s32[16,16]{1,0:T(8,128)}, u32[]{:S(2)}) copy-start(s32[16,16]{1,0:T(8,128)} %param.11) | copy-start | bytes 3076
  4.8 16.7 %copy-start.3 = (f32[8]{0:T(128)S(1)}, f32[8]{0:T(128)}, u32[]{:S(2)}) copy-start(f32[8]{0:T(128)} %param.10) | copy-start | bytes 100
  5.0 22.1 %collective-permute-start.1 = (f32[19,1,16,128]{3,2,1,0:T(8,128)S(1)}, f32[19,1,16,128]{3,2,1,0:T(8,128)S(1)}, u32[]{:S(2)}, u32[]{:S(2)}) collective-permute-start(f32[19,1,16,128]{3,2,1,0:T(8,128)S(1)} %get-tuple-element.48), channel_id=1, source_target_pairs={{16,0},{32,16},{48,32},{64,48},{80,64},{96,80},{112,96},{128,112},... | collective-permute-start | bytes 466952 | tf_op jit(solution)/shard_map/ppermute | solution.py:43
  19.4 17.1 %collective-permute-start = (f32[19,1,16,128]{3,2,1,0:T(8,128)S(1)}, f32[19,1,16,128]{3,2,1,0:T(8,128)S(1)}, u32[]{:S(2)}, u32[]{:S(2)}) collective-permute-start(f32[19,1,16,128]{3,2,1,0:T(8,128)S(1)} %get-tuple-element.47), channel_id=1, source_target_pairs={{0,16},{16,32},{32,48},{48,64},{64,80},{80,96},{96,112},{112,128},... | collective-permute-start | bytes 466952 | tf_op jit(solution)/shard_map/ppermute | solution.py:42
  36.6 11.6 %collective-permute-start.2 = (f32[19,10,1,128]{3,2,1,0:T(1,128)S(1)}, f32[19,10,1,128]{3,2,1,0:T(1,128)S(1)}, u32[]{:S(2)}, u32[]{:S(2)}) collective-permute-start(f32[19,10,1,128]{3,2,1,0:T(1,128)S(1)} %get-tuple-element.39), channel_id=1, source_target_pairs={{0,1},{1,2},{2,3},{3,4},{4,5},{5,6},{6,7},{7,8},{8,9},{9,10},{10,1... | collective-permute-start | bytes 291848 | tf_op jit(solution)/shard_map/ppermute | solution.py:42
  38.5 9.6 %collective-permute-start.3 = (f32[19,10,1,128]{3,2,1,0:T(1,128)S(1)}, f32[19,10,1,128]{3,2,1,0:T(1,128)S(1)}, u32[]{:S(2)}, u32[]{:S(2)}) collective-permute-start(f32[19,10,1,128]{3,2,1,0:T(1,128)S(1)} %get-tuple-element.40), channel_id=1, source_target_pairs={{1,0},{2,1},{3,2},{4,3},{5,4},{6,5},{7,6},{8,7},{9,8},{10,9},{11,1... | collective-permute-start | bytes 291848 | tf_op jit(solution)/shard_map/ppermute | solution.py:43
  49.4 4.4 %collective-permute-start.5 = (f32[3,3,16,128]{3,2,1,0:T(8,128)S(1)}, f32[3,3,16,128]{3,2,1,0:T(8,128)S(1)}, u32[]{:S(2)}, u32[]{:S(2)}) collective-permute-start(f32[3,3,16,128]{3,2,1,0:T(8,128)S(1)} %get-tuple-element.66), channel_id=1, source_target_pairs={{16,0},{32,16},{48,32},{64,48},{80,64},{96,80},{112,96},{128,112},... | collective-permute-start | bytes 221192 | tf_op jit(solution)/shard_map/ppermute | solution.py:43
  51.4 11.7 %collective-permute-start.4 = (f32[3,3,16,128]{3,2,1,0:T(8,128)S(1)}, f32[3,3,16,128]{3,2,1,0:T(8,128)S(1)}, u32[]{:S(2)}, u32[]{:S(2)}) collective-permute-start(f32[3,3,16,128]{3,2,1,0:T(8,128)S(1)} %get-tuple-element.65), channel_id=1, source_target_pairs={{0,16},{16,32},{32,48},{48,64},{64,80},{80,96},{96,112},{112,128},... | collective-permute-start | bytes 221192 | tf_op jit(solution)/shard_map/ppermute | solution.py:42
  63.1 8.9 %collective-permute-start.6 = (f32[3,14,3,128]{3,2,1,0:T(4,128)S(1)}, f32[3,14,3,128]{3,2,1,0:T(4,128)S(1)}, u32[]{:S(2)}, u32[]{:S(2)}) collective-permute-start(f32[3,14,3,128]{3,2,1,0:T(4,128)S(1)} %get-tuple-element.61), channel_id=1, source_target_pairs={{1,0},{2,1},{3,2},{4,3},{5,4},{6,5},{7,6},{8,7},{9,8},{10,9},{11,1... | collective-permute-start | bytes 193544 | tf_op jit(solution)/shard_map/ppermute | solution.py:43
  70.0 9.1 %collective-permute-start.7 = (f32[3,14,3,128]{3,2,1,0:T(4,128)S(1)}, f32[3,14,3,128]{3,2,1,0:T(4,128)S(1)}, u32[]{:S(2)}, u32[]{:S(2)}) collective-permute-start(f32[3,14,3,128]{3,2,1,0:T(4,128)S(1)} %get-tuple-element.62), channel_id=1, source_target_pairs={{0,1},{1,2},{2,3},{3,4},{4,5},{5,6},{6,7},{7,8},{8,9},{9,10},{10,1... | collective-permute-start | bytes 193544 | tf_op jit(solution)/shard_map/ppermute | solution.py:42
  71.9 7.4 %copy-start.1 = (f32[19,8,16,128]{3,2,1,0:T(8,128)}, f32[19,8,16,128]{3,2,1,0:T(8,128)S(1)}, u32[]{:S(2)}) copy-start(f32[19,8,16,128]{3,2,1,0:T(8,128)S(1)} %constant_dynamic-update-slice_fusion.19) | copy-start | bytes 3735556
where the time goes:
time: 83.2 us; the launch traced here: 82.7 us
  starting transfers between devices  37.9 us (46%)
  waiting for transfers between devices  32.3 us (39%)
  other arithmetic  6.87 us (8%)
  local copies, waits for them, and re-layouts  3.75 us (5%)
  between operations  1.79 us (2%)
    ppermute x4, starting transfers between devices, padded_2(): after = lax.ppermute(initial, axis, down)  29.8 us
    ppermute x4, waiting for transfers between devices, padded_2(): before = lax.ppermute(last, axis, up)  28.3 us
    ppermute x4, starting transfers between devices, padded_2(): before = lax.ppermute(last, axis, up)  8.17 us
    ppermute x4, waiting for transfers between devices, padded_2(): after = lax.ppermute(initial, axis, down)  4.02 us
    unnamed x20, other arithmetic  2.35 us
    another operation x2, other arithmetic, per_device(): jnp.stack([jnp.where(shown, weight_x, 0.0), jnp.where(shown, weight_y, 0....  2.03 us
  transfers between devices with their start and end apart: 8, of which 6 were waited for; matrix products, arithmetic and copies ran while one was open for 3% of the time, Pallas kernels for 0%

commit v1 on v0

v1 whole, which is shorter than its diff:
```python
import jax
import jax.numpy as jnp
from jax import lax
from jax.experimental import pallas as pl
from jax.experimental.pallas import tpu as pltpu
from jax.sharding import PartitionSpec as P

BRICK = 16
LEVELS = 8
NXL, NYL, NZL = 8, 16, 128

LATTICE = [
    (0, 0, 0),
    (1, 0, 0),
    (-1, 0, 0),
    (0, 1, 0),
    (0, -1, 0),
    (0, 0, 1),
    (0, 0, -1),
    (1, 1, 0),
    (-1, -1, 0),
    (1, -1, 0),
    (-1, 1, 0),
    (1, 0, 1),
    (-1, 0, -1),
    (1, 0, -1),
    (-1, 0, 1),
    (0, 1, 1),
    (0, -1, -1),
    (0, 1, -1),
    (0, -1, 1),
]
UPWARD = (3, 7, 10, 15, 17)
DOWNWARD = (4, 8, 9, 16, 18)
RIGHTWARD = (1, 7, 9, 11, 13)
LEFTWARD = (2, 8, 10, 12, 14)

Y_MOMENTS = 40
UP_ROWS = (14, 15)
DOWN_ROWS = (0, 1, 2)
Y_LEN = 160
X_LEN = 280
HALO_ROWS = (-2, -1, 16, 17, 18)
PITCH = 32


def edge_start(rows):
    return Y_MOMENTS + 32 * len(rows)


def add(total, value, sign=1):
    if total is None:
        return value if sign == 1 else -value
    return total + value if sign == 1 else total - value


def row_moments(passed, row):
    dens, along_y, along_z = {}, {}, {}
    for number, (cx, cy, cz) in enumerate(LATTICE):
        source = row - cy
        if 0 <= source < NYL:
            tile = passed[number, pl.ds(source, NXL, stride=NYL), :]
            dens[cx] = add(dens.get(cx), tile)
            if cy:
                along_y[cx] = add(along_y.get(cx), tile, cy)
            if cz:
                along_z[cx] = add(along_z.get(cx), tile, cz)
    layer = lax.broadcasted_iota(jnp.int32, (NXL, NZL), 0)
    zero = jnp.zeros((NXL, NZL), jnp.float32)

    def right(tile):
        return zero if tile is None else jnp.where(layer == 0, 0.0, pltpu.roll(tile, 1, 0))

    def left(tile):
        return zero if tile is None else jnp.where(layer == NXL - 1, 0.0, pltpu.roll(tile, NXL - 1, 0))

    def joined(parts):
        return (zero if parts.get(0) is None else parts[0]) + right(parts.get(1)) + left(parts.get(-1))

    tiles = (joined(dens), right(dens.get(1)) - left(dens.get(-1)), joined(along_y), joined(along_z))

    def line(tile, which):
        return jnp.zeros((1, NZL), jnp.float32) if tile is None else tile[which : which + 1]

    beyond = [line(part.get(1), NXL - 1) for part in (dens, along_y, along_z)]
    before = [line(part.get(-1), 0) for part in (dens, along_y, along_z)]
    return tiles, beyond, before


def pack_y(passed, message, numbers, border, rows):
    for place, number in enumerate(numbers):
        message[8 * place : 8 * place + 8, :] = passed[number, pl.ds(border, NXL, stride=NYL), :]
    edge = edge_start(rows)
    for place, row in enumerate(rows):
        tiles, beyond, before = row_moments(passed, row)
        for which in range(4):
            at = Y_MOMENTS + 32 * place + 8 * which
            message[at : at + 8, :] = tiles[which]
        for which in range(3):
            at = edge + 6 * place + which
            message[at : at + 1, :] = beyond[which]
            message[at + 3 : at + 4, :] = before[which]


PAIRS = ((1, (1, 0, 0)), (3, (0, 1, 0)), (5, (0, 0, 1)), (7, (1, 1, 0)), (9, (1, -1, 0)), (11, (1, 0, 1)), (13, (1, 0, -1)), (15, (0, 1, 1)), (17, (0, 1, -1)))


def combine(parts, direction):
    total = None
    for part, sign in zip(parts, direction):
        if sign:
            total = add(total, part, sign)
    return total


def collide_kernel(omega_ref, pop, solid, passed, even_message, odd_message):
    rate = omega_ref[0]
    keep = 1.0 - rate

    def layer(i, carry):
        rows = pl.ds(pl.multiple_of(i * NYL, NYL), NYL)
        own = [pop[number, rows, :] for number in range(19)]
        wall = solid[rows, :] == 1
        differ = {number: own[number] - own[number + 1] for number, _ in PAIRS}
        density = own[0]
        for number, _ in PAIRS:
            density = density + (own[number] + own[number + 1])
        momentum = []
        for axis in range(3):
            total = None
            for number, direction in PAIRS:
                if direction[axis]:
                    total = add(total, differ[number], direction[axis])
            momentum.append(total)
        inverse = 1.0 / density
        velocity = [part * inverse for part in momentum]
        base = 1.0 - 1.5 * (velocity[0] * velocity[0] + velocity[1] * velocity[1] + velocity[2] * velocity[2])
        scale = rate * density
        weight1, weight2 = scale * (1.0 / 18.0), scale * (1.0 / 36.0)
        passed[0, rows, :] = jnp.where(wall, own[0], keep * own[0] + scale * (1.0 / 3.0) * base)
        for number, direction in PAIRS:
            along = combine(velocity, direction)
            weight = weight1 if number < 7 else weight2
            even = base + 4.5 * (along * along)
            odd = 3.0 * along
            plus = jnp.where(wall, own[number + 1], keep * own[number] + weight * (even + odd))
            minus = jnp.where(wall, own[number], keep * own[number + 1] + weight * (even - odd))
            if direction[2]:
                plus = pltpu.roll(plus, direction[2] % NZL, 1)
                minus = pltpu.roll(minus, -direction[2] % NZL, 1)
            passed[number, rows, :] = plus
            passed[number + 1, rows, :] = minus
        return carry

    lax.fori_loop(0, NXL, layer, 0)
    odd_place = lax.axis_index("gy") % 2 == 1

    @pl.when(odd_place)
    def _():
        pack_y(passed, odd_message, UPWARD, NYL - 1, UP_ROWS)
        pack_y(passed, even_message, DOWNWARD, 0, DOWN_ROWS)

    @pl.when(jnp.logical_not(odd_place))
    def _():
        pack_y(passed, even_message, UPWARD, NYL - 1, UP_ROWS)
        pack_y(passed, odd_message, DOWNWARD, 0, DOWN_ROWS)


def chooser(axis, even_message, odd_message):
    odd_place = lax.axis_index(axis) % 2 == 1

    def before(rows):
        return jnp.where(odd_place, even_message[rows, :], odd_message[rows, :])

    def after(rows):
        return jnp.where(odd_place, odd_message[rows, :], even_message[rows, :])

    return before, after


def shifted(tile, fill, step):
    row = lax.broadcasted_iota(jnp.int32, (NYL, NZL), 0)
    if step == 1:
        return jnp.where(row == 0, fill, pltpu.roll(tile, 1, 0))
    return jnp.where(row == NYL - 1, fill, pltpu.roll(tile, NYL - 1, 0))


def padded_at(layer, row):
    return (layer + 1) * PITCH + 8 + row


def moment_kernel(passed, even_in, odd_in, moments, even_out, odd_out):
    before, after = chooser("gy", even_in, odd_in)
    low = {number: before(slice(8 * place, 8 * place + 8)) for place, number in enumerate(UPWARD)}
    high = {number: after(slice(8 * place, 8 * place + 8)) for place, number in enumerate(DOWNWARD)}

    def source(number, layer):
        return passed[number, layer * NYL : (layer + 1) * NYL, :]

    def entering(numbers, signs, layer):
        step = LATTICE[numbers[0]][1]
        lines = low if step == 1 else high
        tile = fill = None
        for number, sign in zip(numbers, signs):
            tile = add(tile, source(number, layer), sign)
            fill = add(fill, lines[number][layer : layer + 1], sign)
        return shifted(tile, fill, step)

    crossing = {}
    sums = {}
    for layer in range(NXL):
        up = entering((3, 15, 17), (1, 1, 1), layer)
        down = entering((4, 16, 18), (1, 1, 1), layer)
        up_z = entering((15, 17), (1, -1), layer)
        down_z = entering((18, 16), (1, -1), layer)
        here5, here6 = source(5, layer), source(6, layer)
        sums[0, layer] = (source(0, layer) + here5 + here6 + up + down, up - down, here5 - here6 + up_z + down_z)
        for side, straight, plus, minus, rise, fall in ((1, 1, 7, 9, 11, 13), (-1, 2, 10, 8, 14, 12)):
            moved_up = entering((plus,), (1,), layer)
            moved_down = entering((minus,), (1,), layer)
            a, b = source(rise, layer), source(fall, layer)
            sums[side, layer] = (source(straight, layer) + a + b + moved_up + moved_down, moved_up - moved_down, a - b)
            if (side, layer) in ((1, NXL - 1), (-1, 0)):
                crossing[plus], crossing[minus] = moved_up, moved_down
    whole = {}
    for layer in range(NXL):
        parts = list(sums[0, layer])
        along_x = None
        if layer > 0:
            parts = [p + q for p, q in zip(parts, sums[1, layer - 1])]
            along_x = sums[1, layer - 1][0]
        if layer < NXL - 1:
            parts = [p + q for p, q in zip(parts, sums[-1, layer + 1])]
            along_x = add(along_x, sums[-1, layer + 1][0], -1)
        whole[layer] = (parts[0], along_x, parts[1], parts[2])
        for which in range(4):
            at = padded_at(layer, 0)
            moments[which, at : at + NYL, :] = whole[layer][which]
    for layer, side in ((-1, -1), (NXL, 1)):
        dens, along_y, along_z = sums[side, 0 if side == -1 else NXL - 1]
        at = padded_at(layer, 0)
        for which, value in enumerate((dens, dens if side == 1 else -dens, along_y, along_z)):
            moments[which, at : at + NYL, :] = value

    def line_of(reader, at):
        return reader(slice(at, at + 1))

    edges = {}
    for row in HALO_ROWS:
        reader, rows, place = (before, UP_ROWS, row + 2) if row < 0 else (after, DOWN_ROWS, row - 16)
        at = Y_MOMENTS + 32 * place
        tiles = [reader(slice(at + 8 * which, at + 8 * which + 8)) for which in range(4)]
        at = edge_start(rows) + 6 * place
        beyond = [line_of(reader, at + which) for which in range(3)]
        ahead = [line_of(reader, at + 3 + which) for which in range(3)]
        if row in (-1, 16):
            own_tiles, own_beyond, own_ahead = row_moments(passed, row)
            tiles = [p + q for p, q in zip(tiles, own_tiles)]
            beyond = [p + q for p, q in zip(beyond, own_beyond)]
            ahead = [p + q for p, q in zip(ahead, own_ahead)]
        for which in range(4):
            moments[which, pl.ds(padded_at(0, row), NXL, stride=PITCH), :] = tiles[which]
        for layer, lines, sign in ((-1, ahead, -1), (NXL, beyond, 1)):
            at = padded_at(layer, row)
            for which, value in enumerate((lines[0], lines[0] if sign == 1 else -lines[0], lines[1], lines[2])):
                moments[which, at : at + 1, :] = value
        edges[row] = (tiles, beyond, ahead)

    def flow_of(parts):
        inverse = 1.0 / parts[0]
        return [part * inverse for part in parts[1:]]

    def put(message, at, values):
        for value in values:
            message[at : at + value.shape[0], :] = value
            at += value.shape[0]

    def line(tiles, layer):
        return [tile[layer : layer + 1] for tile in tiles]

    def pack_right(message):
        last = NXL - 1
        put(message, 0, flow_of(whole[last - 1]))
        put(message, 48, whole[last])
        put(message, 112, [crossing[n] if n in (7, 9) else source(n, last) for n in RIGHTWARD])
        put(message, 192, flow_of(line(edges[16][0], last - 1)) + line(edges[16][0], last) + [v for row in HALO_ROWS for v in edges[row][1]])

    def pack_left(message):
        put(message, 0, whole[0])
        put(message, 64, flow_of(whole[1]) + flow_of(whole[2]))
        put(message, 160, [crossing[n] if n in (8, 10) else source(n, 0) for n in LEFTWARD])
        put(message, 240, [v for row in HALO_ROWS[:4] for v in line(edges[row][0], 0)] + flow_of(line(edges[16][0], 1)) + [v for row in HALO_ROWS for v in edges[row][2]])

    odd_place = lax.axis_index("gx") % 2 == 1

    @pl.when(odd_place)
    def _():
        pack_left(even_out)
        pack_right(odd_out)

    @pl.when(jnp.logical_not(odd_place))
    def _():
        pack_right(even_out)
        pack_left(odd_out)


def passing_kernel(passed, even_in, odd_in, new):
    before, after = chooser("gy", even_in, odd_in)
    low = {number: before(slice(8 * place, 8 * place + 8)) for place, number in enumerate(UPWARD)}
    high = {number: after(slice(8 * place, 8 * place + 8)) for place, number in enumerate(DOWNWARD)}
    for number, (cx, cy, _) in enumerate(LATTICE):
        for layer in range(NXL):
            source = layer - cx
            if not 0 <= source < NXL:
                continue
            tile = passed[number, source * NYL : (source + 1) * NYL, :]
            if cy:
                lines = low if cy == 1 else high
                tile = shifted(tile, lines[number][source : source + 1], cy)
            new[number, layer * NYL : (layer + 1) * NYL, :] = tile


def flow_at(layer, row):
    return (layer + 2) * PITCH + 8 + row


def result_kernel(visible, levels, index, moments, even_in, odd_in, new_in, new, q_field, crossings, flow, sem):
    gx, gy = lax.axis_index("gx"), lax.axis_index("gy")
    odd_place = gx % 2 == 1

    def copies(message, start, numbers, layer):
        return [
            pltpu.make_async_copy(
                message.at[start + NYL * place : start + NYL * (place + 1), :],
                new.at[number, layer * NYL : (layer + 1) * NYL, :],
                sem.at[place],
            )
            for place, number in enumerate(numbers)
        ]

    def from_left(message):
        return copies(message, 112, RIGHTWARD, 0)

    def from_right(message):
        return copies(message, 160, LEFTWARD, NXL - 1)

    def run(left_message, right_message):
        first = from_left(left_message)
        for copy in first:
            copy.start()
        compute(left_message, right_message)
        for copy in first:
            copy.wait()
        second = from_right(right_message)
        for copy in second:
            copy.start()
        for copy in second:
            copy.wait()

    def compute(left_message, right_message):
        def store_flow(layer, row, parts):
            inverse = 1.0 / parts[0]
            at = flow_at(layer, row)
            for axis in range(3):
                flow[axis, at : at + parts[0].shape[0], :] = parts[axis + 1] * inverse

        def own(layer, row, size):
            at = padded_at(layer, row)
            return [moments[which, at : at + size, :] for which in range(4)]

        def both(first, second):
            return [p + q for p, q in zip(first, second)]

        def get(message, at, count, size):
            return [message[at + size * n : at + size * (n + 1), :] for n in range(count)]

        def signed(lines, sign):
            return [lines[0], lines[0] if sign == 1 else -lines[0], lines[1], lines[2]]

        for axis, value in enumerate(get(left_message, 0, 3, NYL)):
            flow[axis, flow_at(-2, 0) : flow_at(-2, NYL), :] = value
        for axis, value in enumerate(get(left_message, 192, 3, 1)):
            flow[axis, flow_at(-2, NYL) : flow_at(-2, NYL) + 1, :] = value
        store_flow(-1, 0, both(get(left_message, 48, 4, NYL), own(-1, 0, NYL)))
        store_flow(-1, NYL, both(get(left_message, 195, 4, 1), own(-1, NYL, 1)))
        n1, n7, n9, n11, n13 = get(left_message, 112, 5, NYL)
        store_flow(0, 0, both(signed([n1 + n7 + n9 + n11 + n13, n7 - n9, n11 - n13], 1), own(0, 0, NYL)))
        for place, row in enumerate(HALO_ROWS):
            store_flow(0, row, both(signed(get(left_message, 199 + 3 * place, 3, 1), 1), own(0, row, 1)))
        for layer in range(1, NXL - 1):
            store_flow(layer, -8, own(layer, -8, PITCH))
        n2, n8, n10, n12, n14 = get(right_message, 160, 5, NYL)
        store_flow(NXL - 1, 0, both(signed([n2 + n8 + n10 + n12 + n14, n10 - n8, n14 - n12], -1), own(NXL - 1, 0, NYL)))
        for place, row in enumerate(HALO_ROWS):
            store_flow(NXL - 1, row, both(signed(get(right_message, 259 + 3 * place, 3, 1), -1), own(NXL - 1, row, 1)))
        store_flow(NXL, 0, both(get(right_message, 0, 4, NYL), own(NXL, 0, NYL)))
        for place, row in enumerate(HALO_ROWS[:4]):
            store_flow(NXL, row, both(get(right_message, 240 + 4 * place, 4, 1), own(NXL, row, 1)))
        for axis, value in enumerate(get(right_message, 64, 3, NYL)):
            flow[axis, flow_at(NXL + 1, 0) : flow_at(NXL + 1, NYL), :] = value
        for axis, value in enumerate(get(right_message, 256, 3, 1)):
            flow[axis, flow_at(NXL + 1, NYL) : flow_at(NXL + 1, NYL) + 1, :] = value
        for axis, value in enumerate(get(right_message, 112, 3, NYL)):
            flow[axis, flow_at(NXL + 2, 0) : flow_at(NXL + 2, NYL), :] = value

        def stencil(minus2, minus1, plus1, plus2):
            return 8.0 * (plus1 - minus1) + (minus2 - plus2)

        def scaled_at(load):
            grads = []
            for axis in range(3):
                centre = load(axis, 0, 0)
                grads.append(
                    (
                        stencil(*[load(axis, d, 0) for d in (-2, -1, 1, 2)]),
                        stencil(*[load(axis, 0, d) for d in (-2, -1, 1, 2)]),
                        stencil(*[pltpu.roll(centre, -d % NZL, 1) for d in (-2, -1, 1, 2)]),
                    )
                )
            inner = grads[0][0] * grads[0][0] + grads[1][1] * grads[1][1] + grads[2][2] * grads[2][2]
            inner = inner + 2.0 * (grads[0][1] * grads[1][0] + grads[0][2] * grads[2][0] + grads[1][2] * grads[2][1])
            return inner * (-50.0 / 144.0)

        def layer_load(layer):
            def load(axis, dx, dy):
                at = flow_at(layer + dx, dy)
                return flow[axis, at : at + NYL, :]

            return load

        def row_load(axis, dx, dy):
            return flow[axis, pl.ds(flow_at(dx, NYL + dy), NXL, stride=PITCH), :]

        level = levels[index[gx * NXL // BRICK, gy * NYL // BRICK]]
        lane = lax.broadcasted_iota(jnp.int32, (NYL, NZL), 1) // BRICK
        shown = jnp.zeros((NYL, NZL), jnp.int32)
        for brick in range(NZL // BRICK):
            shown = jnp.where(lane == brick, visible[gx * NXL // BRICK, gy * NYL // BRICK, brick], shown)
        shown = shown == 1

        def crossing(here, there):
            return jnp.where(shown, jnp.maximum(-here * there, 0.0) / (here * here + there * there + 0.25), 0.0)

        above = scaled_at(row_load)
        following = scaled_at(layer_load(0))
        for layer in range(NXL):
            scaled, following = following, scaled_at(layer_load(layer + 1))
            at = layer * NYL
            here = scaled - level
            q_field[at : at + NYL, :] = jnp.where(shown, scaled, 0.0)
            crossings[0, at : at + NYL, :] = crossing(here, following - level)
            crossings[1, at : at + NYL, :] = crossing(here, shifted(scaled, above[layer : layer + 1], -1) - level)
            crossings[2, at : at + NYL, :] = crossing(here, pltpu.roll(here, NZL - 1, 1))

    @pl.when(odd_place)
    def _():
        run(even_in, odd_in)

    @pl.when(jnp.logical_not(odd_place))
    def _():
        run(odd_in, even_in)


def swap(value, axis, parity):
    size = lax.axis_size(axis)
    pairs = []
    for i in range(size):
        mate = i + 1 if i % 2 == parity else i - 1
        pairs.append((i, mate % size))
    return lax.ppermute(value, axis, pairs)


VMEM = pl.BlockSpec(memory_space=pltpu.VMEM)
SMEM = pl.BlockSpec(memory_space=pltpu.SMEM)
ANY = pl.BlockSpec(memory_space=pl.ANY)


def shape(*dims):
    return jax.ShapeDtypeStruct(dims, jnp.float32)


def per_device(populations, solid, visible, omega, iso_levels, iso_index):
    cells = NXL * NYL
    passed, to_even, to_odd = pl.pallas_call(
        collide_kernel,
        out_shape=(shape(19, cells, NZL), shape(Y_LEN, NZL), shape(Y_LEN, NZL)),
        in_specs=[SMEM, VMEM, VMEM],
        out_specs=(VMEM, VMEM, VMEM),
    )(omega, populations.reshape(19, cells, NZL), solid.reshape(cells, NZL))
    odd_y = swap(to_odd, "gy", 1)
    even_y = swap(to_even, "gy", 0)
    moments, to_even, to_odd = pl.pallas_call(
        moment_kernel,
        out_shape=(shape(4, (NXL + 2) * PITCH, NZL), shape(X_LEN, NZL), shape(X_LEN, NZL)),
        in_specs=[VMEM, VMEM, VMEM],
        out_specs=(VMEM, VMEM, VMEM),
    )(passed, even_y, odd_y)
    odd_x = swap(to_odd, "gx", 1)
    even_x = swap(to_even, "gx", 0)
    new = pl.pallas_call(
        passing_kernel,
        out_shape=shape(19, cells, NZL),
        in_specs=[VMEM, VMEM, VMEM],
        out_specs=VMEM,
    )(passed, even_y, odd_y)
    new, q_field, crossings = pl.pallas_call(
        result_kernel,
        out_shape=(shape(19, cells, NZL), shape(cells, NZL), shape(3, cells, NZL)),
        in_specs=[SMEM, SMEM, SMEM, VMEM, VMEM, VMEM, ANY],
        out_specs=(ANY, VMEM, VMEM),
        scratch_shapes=[pltpu.VMEM((3, (NXL + 5) * PITCH, NZL), jnp.float32), pltpu.SemaphoreType.DMA((5,))],
        input_output_aliases={6: 0},
    )(visible, iso_levels, iso_index, moments, even_x, odd_x, new)
    return (
        new.reshape(19, NXL, NYL, NZL),
        q_field.reshape(NXL, NYL, NZL),
        crossings.reshape(3, NXL, NYL, NZL),
    )


def solution(mesh):
    in_specs = (P(None, "gx", "gy", None), P("gx", "gy", None), P(), P(), P(), P())
    out_specs = (P(None, "gx", "gy", None), P("gx", "gy", None), P(None, "gx", "gy", None))
    return jax.shard_map(
        per_device, mesh=mesh, in_specs=in_specs, out_specs=out_specs, check_vma=False
    )
```

time: 83.2 us -> 50.8 us (0.61)
  the two profiles are of different devices: /device:TPU:16 before, /device:TPU:24 now
where the time goes in v1:
time: 50.8 us; the launch traced here: 50.5 us
  starting transfers between devices  24.7 us (49%)
  Pallas kernels  14.1 us (28%)
  waiting for transfers between devices  8.32 us (16%)
  local copies, waits for them, and re-layouts  2.03 us (4%)
  between operations  1.35 us (3%)
    ppermute x4, starting transfers between devices, swap(): return lax.ppermute(value, axis, pairs)  24.7 us
    ppermute x4, waiting for transfers between devices, swap(): return lax.ppermute(value, axis, pairs)  8.32 us
    pallas_call x1, Pallas kernels, per_device(): pl.pallas_call(result_kernel, out_shape=(shape(19, cells, NZL), shape(cel...  5.51 us
    pallas_call x1, Pallas kernels, per_device(): pl.pallas_call(collide_kernel, out_shape=(shape(19, cells, NZL), shape(Y_...  3.63 us
    pallas_call x1, Pallas kernels, per_device(): pl.pallas_call(moment_kernel, out_shape=(shape(4, (NXL + 2) * PITCH, NZL)...  2.54 us
    pallas_call x1, Pallas kernels, per_device(): pl.pallas_call(passing_kernel, out_shape=shape(19, cells, NZL), in_specs=...  2.47 us
    unnamed x11, local copies, waits for them, and re-layouts  2.03 us
  transfers between devices with their start and end apart: 4, of which 2 were waited for; matrix products, arithmetic and copies ran while one was open for 1% of the time, Pallas kernels for 5%

profile of v1, /device:TPU:24, one launch (start us, length us, event | category | flops | bytes accessed | tf_op | source)
XLA Modules:
  0.0 50.5 jit_solution(7600134766920618080)
XLA Ops:
  1.3 0.0 copy-start.4
  1.3 3.6 %shard_map.85 = (f32[19,128,128]{2,1,0:T(8,128)}, f32[160,128]{1,0:T(8,128)}, f32[160,128]{1,0:T(8,128)}) custom-call(f32[1]{0:T(128)S(6)} %copy.12.omega_ref, f32[19,128,128]{2,1,0:T(8,128)} %bitcast.6, s32[128,128]{1,0:T(8,128)} %bitcast.7), custom_call_target="tpu_custom_call" | custom-call | tf_op jit(solution)/shard_map/pallas_call | solution.py:484
  4.9 3.8 %collective-permute-start = (f32[160,128]{1,0:T(8,128)}, f32[160,128]{1,0:T(8,128)S(1)}, u32[]{:S(2)}, u32[]{:S(2)}) collective-permute-start(f32[160,128]{1,0:T(8,128)} %get-tuple-element.13), channel_id=1, source_target_pairs={{0,1},{1,0},{2,3},{3,2},{4,5},{5,4},{6,7},{7,6},{8,9},{9,8},{10,11... | collective-permute-start | bytes 245768 | tf_op jit(solution)/shard_map/ppermute | solution.py:470
  8.7 4.9 %collective-permute-start.1 = (f32[160,128]{1,0:T(8,128)}, f32[160,128]{1,0:T(8,128)S(1)}, u32[]{:S(2)}, u32[]{:S(2)}) collective-permute-start(f32[160,128]{1,0:T(8,128)} %get-tuple-element.14), channel_id=1, source_target_pairs={{0,15},{1,2},{2,1},{3,4},{4,3},{5,6},{6,5},{7,8},{8,7},{9,10},{10,... | collective-permute-start | bytes 245768 | tf_op jit(solution)/shard_map/ppermute | solution.py:470
  13.6 0.0 collective-permute-done.even_in
  13.7 0.0 copy-start
  13.7 4.4 %collective-permute-done.1.odd_in = f32[160,128]{1,0:T(8,128)S(1)} collective-permute-done((f32[160,128]{1,0:T(8,128)}, f32[160,128]{1,0:T(8,128)S(1)}, u32[]{:S(2)}, u32[]{:S(2)}) %collective-permute-start.1) | collective-permute-done | bytes 81952 | tf_op jit(solution)/shard_map/ppermute | solution.py:470
  18.1 0.0 copy-start.1
  18.1 0.0 copy-done
  18.1 0.6 %copy-done.1 = f32[160,128]{1,0:T(8,128)} copy-done((f32[160,128]{1,0:T(8,128)}, f32[160,128]{1,0:T(8,128)S(1)}, u32[]{:S(2)}) %copy-start.1) | copy-done | bytes 81944
  18.7 2.5 %shard_map.86 = (f32[4,320,128]{2,1,0:T(8,128)}, f32[280,128]{1,0:T(8,128)}, f32[280,128]{1,0:T(8,128)}) custom-call(f32[19,128,128]{2,1,0:T(8,128)} %get-tuple-element.12.passed, f32[160,128]{1,0:T(8,128)} %copy-done, f32[160,128]{1,0:T(8,128)} %copy-done.1), custom_call_target="tpu_custom_call" | custom-call | tf_op jit(solution)/shard_map/pallas_call | solution.py:492
  21.3 1.9 %collective-permute-start.2 = (f32[280,128]{1,0:T(8,128)}, f32[280,128]{1,0:T(8,128)S(1)}, u32[]{:S(2)}, u32[]{:S(2)}) collective-permute-start(f32[280,128]{1,0:T(8,128)} %get-tuple-element.16), channel_id=1, source_target_pairs={{0,16},{16,0},{32,48},{48,32},{64,80},{80,64},{96,112},{112,96},{1... | collective-permute-start | bytes 430088 | tf_op jit(solution)/shard_map/ppermute | solution.py:470
  23.2 14.0 %collective-permute-start.3 = (f32[280,128]{1,0:T(8,128)}, f32[280,128]{1,0:T(8,128)S(1)}, u32[]{:S(2)}, u32[]{:S(2)}) collective-permute-start(f32[280,128]{1,0:T(8,128)} %get-tuple-element.17), channel_id=1, source_target_pairs={{0,496},{16,32},{32,16},{48,64},{64,48},{80,96},{96,80},{112,128},... | collective-permute-start | bytes 430088 | tf_op jit(solution)/shard_map/ppermute | solution.py:470
  37.2 0.0 copy-done.4
  37.2 0.8 %copy.10.visible = s32[16,16,8]{2,1,0:T(8,128)} copy(s32[16,16,8]{1,2,0:T(8,128)S(1)} %copy-done.4) | data formatting | bytes 16384 | tf_op args[2]
  38.0 2.5 %shard_map.87.new_in = f32[19,128,128]{2,1,0:T(8,128)} custom-call(f32[19,128,128]{2,1,0:T(8,128)} %get-tuple-element.12.passed, f32[160,128]{1,0:T(8,128)} %copy-done, f32[160,128]{1,0:T(8,128)} %copy-done.1), custom_call_target="tpu_custom_call" | custom-call | tf_op jit(solution)/shard_map/pallas_call | solution.py:500
  40.4 0.0 collective-permute-done.2.even_in
  40.4 0.0 copy-start.2
  40.4 3.9 %collective-permute-done.3.odd_in = f32[280,128]{1,0:T(8,128)S(1)} collective-permute-done((f32[280,128]{1,0:T(8,128)}, f32[280,128]{1,0:T(8,128)S(1)}, u32[]{:S(2)}, u32[]{:S(2)}) %collective-permute-start.3) | collective-permute-done | bytes 143392 | tf_op jit(solution)/shard_map/ppermute | solution.py:470
  44.3 0.0 copy-start.3
  44.3 0.0 copy-done.2
  44.3 0.6 %copy-done.3 = f32[280,128]{1,0:T(8,128)} copy-done((f32[280,128]{1,0:T(8,128)}, f32[280,128]{1,0:T(8,128)S(1)}, u32[]{:S(2)}) %copy-start.3) | copy-done | bytes 143384
  45.0 5.5 %shard_map.88 = (f32[19,128,128]{2,1,0:T(8,128)}, f32[128,128]{1,0:T(8,128)}, f32[3,128,128]{2,1,0:T(8,128)}) custom-call(s32[16,16,8]{2,1,0:T(8,128)} %copy.10.visible, f32[8]{0:T(128)} %levels.1, s32[16,16]{1,0:T(8,128)} %index.1, f32[4,320,128]{2,1,0:T(8,128)} %get-tuple-element.15.moments, ...), custom_call_target="tpu_custom_call", output_to_operand_aliasing={{0}: (6, {})} | custom-call | tf_op jit(solution)/shard_map/pallas_call | solution.py:506
Async XLA Ops:
  1.3 35.9 %copy-start.4 = (s32[16,16,8]{1,2,0:T(8,128)S(1)}, s32[16,16,8]{1,2,0:T(8,128)}, u32[]{:S(2)}) copy-start(s32[16,16,8]{1,2,0:T(8,128)} %param.8) | copy-start | bytes 24580
  4.9 8.7 %collective-permute-start = (f32[160,128]{1,0:T(8,128)}, f32[160,128]{1,0:T(8,128)S(1)}, u32[]{:S(2)}, u32[]{:S(2)}) collective-permute-start(f32[160,128]{1,0:T(8,128)} %get-tuple-element.13), channel_id=1, source_target_pairs={{0,1},{1,0},{2,3},{3,2},{4,5},{5,4},{6,7},{7,6},{8,9},{9,8},{10,11... | collective-permute-start | bytes 245768 | tf_op jit(solution)/shard_map/ppermute | solution.py:470
  8.7 9.3 %collective-permute-start.1 = (f32[160,128]{1,0:T(8,128)}, f32[160,128]{1,0:T(8,128)S(1)}, u32[]{:S(2)}, u32[]{:S(2)}) collective-permute-start(f32[160,128]{1,0:T(8,128)} %get-tuple-element.14), channel_id=1, source_target_pairs={{0,15},{1,2},{2,1},{3,4},{4,3},{5,6},{6,5},{7,8},{8,7},{9,10},{10,... | collective-permute-start | bytes 245768 | tf_op jit(solution)/shard_map/ppermute | solution.py:470
  13.7 4.4 %copy-start = (f32[160,128]{1,0:T(8,128)}, f32[160,128]{1,0:T(8,128)S(1)}, u32[]{:S(2)}) copy-start(f32[160,128]{1,0:T(8,128)S(1)} %collective-permute-done.even_in) | copy-start | bytes 245764
  18.1 0.6 %copy-start.1 = (f32[160,128]{1,0:T(8,128)}, f32[160,128]{1,0:T(8,128)S(1)}, u32[]{:S(2)}) copy-start(f32[160,128]{1,0:T(8,128)S(1)} %collective-permute-done.1.odd_in) | copy-start | bytes 245764
  21.3 19.2 %collective-permute-start.2 = (f32[280,128]{1,0:T(8,128)}, f32[280,128]{1,0:T(8,128)S(1)}, u32[]{:S(2)}, u32[]{:S(2)}) collective-permute-start(f32[280,128]{1,0:T(8,128)} %get-tuple-element.16), channel_id=1, source_target_pairs={{0,16},{16,0},{32,48},{48,32},{64,80},{80,64},{96,112},{112,96},{1... | collective-permute-start | bytes 430088 | tf_op jit(solution)/shard_map/ppermute | solution.py:470
  23.2 21.2 %collective-permute-start.3 = (f32[280,128]{1,0:T(8,128)}, f32[280,128]{1,0:T(8,128)S(1)}, u32[]{:S(2)}, u32[]{:S(2)}) collective-permute-start(f32[280,128]{1,0:T(8,128)} %get-tuple-element.17), channel_id=1, source_target_pairs={{0,496},{16,32},{32,16},{48,64},{64,48},{80,96},{96,80},{112,128},... | collective-permute-start | bytes 430088 | tf_op jit(solution)/shard_map/ppermute | solution.py:470
  40.4 3.9 %copy-start.2 = (f32[280,128]{1,0:T(8,128)}, f32[280,128]{1,0:T(8,128)S(1)}, u32[]{:S(2)}) copy-start(f32[280,128]{1,0:T(8,128)S(1)} %collective-permute-done.2.even_in) | copy-start | bytes 430084
  44.3 0.6 %copy-start.3 = (f32[280,128]{1,0:T(8,128)}, f32[280,128]{1,0:T(8,128)S(1)}, u32[]{:S(2)}) copy-start(f32[280,128]{1,0:T(8,128)S(1)} %collective-permute-done.3.odd_in) | copy-start | bytes 430084

commit v2 on v1

--- a/solution.py
+++ b/solution.py
@@ -55,11 +55,20 @@
 
 
 def row_moments(passed, row):
+    return tile_moments(
+        {
+            number: passed[number, pl.ds(row - cy, NXL, stride=NYL), :]
+            for number, (_, cy, _) in enumerate(LATTICE)
+            if 0 <= row - cy < NYL
+        }
+    )
+
+
+def tile_moments(tiles):
     dens, along_y, along_z = {}, {}, {}
     for number, (cx, cy, cz) in enumerate(LATTICE):
-        source = row - cy
-        if 0 <= source < NYL:
-            tile = passed[number, pl.ds(source, NXL, stride=NYL), :]
+        if number in tiles:
+            tile = tiles[number]
             dens[cx] = add(dens.get(cx), tile)
             if cy:
                 along_y[cx] = add(along_y.get(cx), tile, cy)
@@ -113,11 +122,24 @@
     return total
 
 
-def collide_kernel(omega_ref, pop, solid, passed, even_message, odd_message):
+def collide_kernel(omega_ref, pop_in, solid_in, passed, odd_message, even_message, pop, solid, sem):
     rate = omega_ref[0]
     keep = 1.0 - rate
 
+    def loads(i):
+        rows = pl.ds(pl.multiple_of(i * NYL, NYL), NYL)
+        return (
+            pltpu.make_async_copy(pop_in.at[:, rows, :], pop.at[:, rows, :], sem.at[0, i]),
+            pltpu.make_async_copy(solid_in.at[rows, :], solid.at[rows, :], sem.at[1, i]),
+        )
+
+    for i in range(NXL):
+        for copy in loads(i):
+            copy.start()
+
     def layer(i, carry):
+        for copy in loads(i):
+            copy.wait()
         rows = pl.ds(pl.multiple_of(i * NYL, NYL), NYL)
         own = [pop[number, rows, :] for number in range(19)]
         wall = solid[rows, :] == 1
@@ -125,13 +147,7 @@
         density = own[0]
         for number, _ in PAIRS:
             density = density + (own[number] + own[number + 1])
-        momentum = []
-        for axis in range(3):
-            total = None
-            for number, direction in PAIRS:
-                if direction[axis]:
-                    total = add(total, differ[number], direction[axis])
-            momentum.append(total)
+        momentum = [combine([differ[number] for number, _ in PAIRS], [d[axis] for _, d in PAIRS]) for axis in range(3)]
         inverse = 1.0 / density
         velocity = [part * inverse for part in momentum]
         base = 1.0 - 1.5 * (velocity[0] * velocity[0] + velocity[1] * velocity[1] + velocity[2] * velocity[2])
@@ -189,63 +205,92 @@
     return (layer + 1) * PITCH + 8 + row
 
 
-def moment_kernel(passed, even_in, odd_in, moments, even_out, odd_out):
-    before, after = chooser("gy", even_in, odd_in)
-    low = {number: before(slice(8 * place, 8 * place + 8)) for place, number in enumerate(UPWARD)}
-    high = {number: after(slice(8 * place, 8 * place + 8)) for place, number in enumerate(DOWNWARD)}
-
+def moment_kernel(passed, moments):
     def source(number, layer):
         return passed[number, layer * NYL : (layer + 1) * NYL, :]
 
     def entering(numbers, signs, layer):
-        step = LATTICE[numbers[0]][1]
-        lines = low if step == 1 else high
-        tile = fill = None
+        tile = None
         for number, sign in zip(numbers, signs):
             tile = add(tile, source(number, layer), sign)
-            fill = add(fill, lines[number][layer : layer + 1], sign)
-        return shifted(tile, fill, step)
-
-    crossing = {}
-    sums = {}
-    for layer in range(NXL):
+        return shifted(tile, 0.0, LATTICE[numbers[0]][1])
+
+    def own_sums(layer):
         up = entering((3, 15, 17), (1, 1, 1), layer)
         down = entering((4, 16, 18), (1, 1, 1), layer)
         up_z = entering((15, 17), (1, -1), layer)
         down_z = entering((18, 16), (1, -1), layer)
         here5, here6 = source(5, layer), source(6, layer)
-        sums[0, layer] = (source(0, layer) + here5 + here6 + up + down, up - down, here5 - here6 + up_z + down_z)
-        for side, straight, plus, minus, rise, fall in ((1, 1, 7, 9, 11, 13), (-1, 2, 10, 8, 14, 12)):
-            moved_up = entering((plus,), (1,), layer)
-            moved_down = entering((minus,), (1,), layer)
-            a, b = source(rise, layer), source(fall, layer)
-            sums[side, layer] = (source(straight, layer) + a + b + moved_up + moved_down, moved_up - moved_down, a - b)
-            if (side, layer) in ((1, NXL - 1), (-1, 0)):
-                crossing[plus], crossing[minus] = moved_up, moved_down
-    whole = {}
+        return (source(0, layer) + here5 + here6 + up + down, up - down, here5 - here6 + up_z + down_z)
+
+    def side_sums(layer, straight, plus, minus, rise, fall):
+        moved_up = entering((plus,), (1,), layer)
+        moved_down = entering((minus,), (1,), layer)
+        a, b = source(rise, layer), source(fall, layer)
+        return (source(straight, layer) + a + b + moved_up + moved_down, moved_up - moved_down, a - b)
+
+    def to_right(layer):
+        return side_sums(layer, 1, 7, 9, 11, 13)
+
+    def to_left(layer):
+        return side_sums(layer, 2, 10, 8, 14, 12)
+
+    def store(layer, values):
+        at = padded_at(layer, 0)
+        for which in range(4):
+            moments[which, at : at + NYL, :] = values[which]
+
     for layer in range(NXL):
-        parts = list(sums[0, layer])
-        along_x = None
+        parts, along_x = list(own_sums(layer)), None
         if layer > 0:
-            parts = [p + q for p, q in zip(parts, sums[1, layer - 1])]
-            along_x = sums[1, layer - 1][0]
+            extra = to_right(layer - 1)
+            parts, along_x = [p + q for p, q in zip(parts, extra)], extra[0]
         if layer < NXL - 1:
-            parts = [p + q for p, q in zip(parts, sums[-1, layer + 1])]
-            along_x = add(along_x, sums[-1, layer + 1][0], -1)
-        whole[layer] = (parts[0], along_x, parts[1], parts[2])
-        for which in range(4):
-            at = padded_at(layer, 0)
-            moments[which, at : at + NYL, :] = whole[layer][which]
-    for layer, side in ((-1, -1), (NXL, 1)):
-        dens, along_y, along_z = sums[side, 0 if side == -1 else NXL - 1]
-        at = padded_at(layer, 0)
-        for which, value in enumerate((dens, dens if side == 1 else -dens, along_y, along_z)):
-            moments[which, at : at + NYL, :] = value
+            extra = to_left(layer + 1)
+            parts, along_x = [p + q for p, q in zip(parts, extra)], add(along_x, extra[0], -1)
+        store(layer, (parts[0], along_x, parts[1], parts[2]))
+    dens, along_y, along_z = to_left(0)
+    store(-1, (dens, -dens, along_y, along_z))
+    dens, along_y, along_z = to_right(NXL - 1)
+    store(NXL, (dens, dens, along_y, along_z))
+    for row in (-1, NYL):
+        tiles, beyond, ahead = row_moments(passed, row)
+        store_row(moments, row, tiles, beyond, ahead)
+
+
+def store_row(moments, row, tiles, beyond, ahead):
+    for which in range(4):
+        moments[which, pl.ds(padded_at(0, row), NXL, stride=PITCH), :] = tiles[which]
+    for layer, lines, sign in ((-1, ahead, -1), (NXL, beyond, 1)):
+        at = padded_at(layer, row)
+        for which, value in enumerate((lines[0], lines[0] if sign == 1 else -lines[0], lines[1], lines[2])):
+            moments[which, at : at + 1, :] = value
+
+
+def load_row(moments, row):
+    tiles = [moments[which, pl.ds(padded_at(0, row), NXL, stride=PITCH), :] for which in range(4)]
+    beyond, ahead = (
+        [moments[which, padded_at(layer, row) : padded_at(layer, row) + 1, :] for which in (0, 2, 3)]
+        for layer in (NXL, -1)
+    )
+    return tiles, beyond, ahead
+
+
+def joining_kernel(passed, odd_in, even_in, moments_in, moments, odd_out, even_out):
+    moments[...] = moments_in[...]
+    before, after = chooser("gy", even_in, odd_in)
+    low = {number: before(slice(8 * place, 8 * place + 8)) for place, number in enumerate(UPWARD)}
+    high = {number: after(slice(8 * place, 8 * place + 8)) for place, number in enumerate(DOWNWARD)}
 
     def line_of(reader, at):
         return reader(slice(at, at + 1))
 
+    def sums(first, second):
+        return [[p + q for p, q in zip(a, b)] for a, b in zip(first, second)]
+
     edges = {}
+    for row, lines in ((0, low), (NYL - 1, high)):
+        store_row(moments, row, *sums(load_row(moments, row), tile_moments(lines)))
     for row in HALO_ROWS:
         reader, rows, place = (before, UP_ROWS, row + 2) if row < 0 else (after, DOWN_ROWS, row - 16)
         at = Y_MOMENTS + 32 * place
@@ -254,16 +299,8 @@
         beyond = [line_of(reader, at + which) for which in range(3)]
         ahead = [line_of(reader, at + 3 + which) for which in range(3)]
         if row in (-1, 16):
-            own_tiles, own_beyond, own_ahead = row_moments(passed, row)
-            tiles = [p + q for p, q in zip(tiles, own_tiles)]
-            beyond = [p + q for p, q in zip(beyond, own_beyond)]
-            ahead = [p + q for p, q in zip(ahead, own_ahead)]
-        for which in range(4):
-            moments[which, pl.ds(padded_at(0, row), NXL, stride=PITCH), :] = tiles[which]
-        for layer, lines, sign in ((-1, ahead, -1), (NXL, beyond, 1)):
-            at = padded_at(layer, row)
-            for which, value in enumerate((lines[0], lines[0] if sign == 1 else -lines[0], lines[1], lines[2])):
-                moments[which, at : at + 1, :] = value
+            tiles, beyond, ahead = sums(load_row(moments, row), (tiles, beyond, ahead))
+        store_row(moments, row, tiles, beyond, ahead)
         edges[row] = (tiles, beyond, ahead)
 
     def flow_of(parts):
@@ -278,33 +315,44 @@
     def line(tiles, layer):
         return [tile[layer : layer + 1] for tile in tiles]
 
+    def whole(layer):
+        at = padded_at(layer, 0)
+        return [moments[which, at : at + NYL, :] for which in range(4)]
+
+    def leaving(number, layer):
+        tile = passed[number, layer * NYL : (layer + 1) * NYL, :]
+        cy = LATTICE[number][1]
+        if cy:
+            tile = shifted(tile, (low if cy == 1 else high)[number][layer : layer + 1], cy)
+        return tile
+
     def pack_right(message):
         last = NXL - 1
-        put(message, 0, flow_of(whole[last - 1]))
-        put(message, 48, whole[last])
-        put(message, 112, [crossing[n] if n in (7, 9) else source(n, last) for n in RIGHTWARD])
+        put(message, 0, flow_of(whole(last - 1)))
+        put(message, 48, whole(last))
+        put(message, 112, [leaving(number, last) for number in RIGHTWARD])
         put(message, 192, flow_of(line(edges[16][0], last - 1)) + line(edges[16][0], last) + [v for row in HALO_ROWS for v in edges[row][1]])
 
     def pack_left(message):
-        put(message, 0, whole[0])
-        put(message, 64, flow_of(whole[1]) + flow_of(whole[2]))
-        put(message, 160, [crossing[n] if n in (8, 10) else source(n, 0) for n in LEFTWARD])
+        put(message, 0, whole(0))
+        put(message, 64, flow_of(whole(1)) + flow_of(whole(2)))
+        put(message, 160, [leaving(number, 0) for number in LEFTWARD])
         put(message, 240, [v for row in HALO_ROWS[:4] for v in line(edges[row][0], 0)] + flow_of(line(edges[16][0], 1)) + [v for row in HALO_ROWS for v in edges[row][2]])
 
     odd_place = lax.axis_index("gx") % 2 == 1
 
     @pl.when(odd_place)
     def _():
+        pack_right(odd_out)
         pack_left(even_out)
-        pack_right(odd_out)
 
     @pl.when(jnp.logical_not(odd_place))
     def _():
+        pack_left(odd_out)
         pack_right(even_out)
-        pack_left(odd_out)
-
-
-def passing_kernel(passed, even_in, odd_in, new):
+
+
+def passing_kernel(visible, levels, index, passed, odd_in, even_in, moments, new, flow, shades):
     before, after = chooser("gy", even_in, odd_in)
     low = {number: before(slice(8 * place, 8 * place + 8)) for place, number in enumerate(UPWARD)}
     high = {number: after(slice(8 * place, 8 * place + 8)) for place, number in enumerate(DOWNWARD)}
@@ -318,46 +366,61 @@
                 lines = low if cy == 1 else high
                 tile = shifted(tile, lines[number][source : source + 1], cy)
             new[number, layer * NYL : (layer + 1) * NYL, :] = tile
+    for layer in range(1, NXL - 1):
+        at = padded_at(layer, -8)
+        inverse = 1.0 / moments[0, at : at + PITCH, :]
+        to = flow_at(layer, -8)
+        for axis in range(3):
+            flow[axis, to : to + PITCH, :] = moments[axis + 1, at : at + PITCH, :] * inverse
+    brick_x, brick_y = lax.axis_index("gx") * NXL // BRICK, lax.axis_index("gy") * NYL // BRICK
+    lane = lax.broadcasted_iota(jnp.int32, (8, NZL), 1) // BRICK
+    shown = jnp.zeros((8, NZL), jnp.int32)
+    for brick in range(NZL // BRICK):
+        shown = jnp.where(lane == brick, visible[brick_x, brick, brick_y], shown)
+    shades[0:8, :] = shown.astype(jnp.float32)
+    shades[8:16, :] = jnp.full((8, NZL), levels[index[brick_x, brick_y]], jnp.float32)
 
 
 def flow_at(layer, row):
     return (layer + 2) * PITCH + 8 + row
 
 
-def result_kernel(visible, levels, index, moments, even_in, odd_in, new_in, new, q_field, crossings, flow, sem):
-    gx, gy = lax.axis_index("gx"), lax.axis_index("gy")
-    odd_place = gx % 2 == 1
-
-    def copies(message, start, numbers, layer):
+def result_kernel(shades, moments, odd_in, even_in, inner_flow, new_in, new, q_field, crossings, outer_flow, q_held, c_held, sem, out_sem):
+    del new_in
+    odd_place = lax.axis_index("gx") % 2 == 1
+
+    def copies(message, start, numbers, layer, first):
         return [
             pltpu.make_async_copy(
                 message.at[start + NYL * place : start + NYL * (place + 1), :],
                 new.at[number, layer * NYL : (layer + 1) * NYL, :],
-                sem.at[place],
+                sem.at[first + place],
             )
             for place, number in enumerate(numbers)
         ]
 
-    def from_left(message):
-        return copies(message, 112, RIGHTWARD, 0)
-
-    def from_right(message):
-        return copies(message, 160, LEFTWARD, NXL - 1)
-
     def run(left_message, right_message):
-        first = from_left(left_message)
-        for copy in first:
+        copied = copies(left_message, 112, RIGHTWARD, 0, 0) + copies(right_message, 160, LEFTWARD, NXL - 1, 5)
+        for copy in copied:
             copy.start()
-        compute(left_message, right_message)
-        for copy in first:
+        copied += compute(left_message, right_message)
+        for copy in copied:
             copy.wait()
-        second = from_right(right_message)
-        for copy in second:
-            copy.start()
-        for copy in second:
-            copy.wait()
+
+    def stores(layer):
+        rows = slice(layer * NYL, (layer + 2) * NYL)
+        return [
+            pltpu.make_async_copy(q_held.at[rows, :], q_field.at[rows, :], out_sem.at[0, layer // 2]),
+            pltpu.make_async_copy(c_held.at[:, rows, :], crossings.at[:, rows, :], out_sem.at[1, layer // 2]),
+        ]
+
+    def flow_ref(layer):
+        return inner_flow if 0 < layer < NXL - 1 else outer_flow
 
     def compute(left_message, right_message):
+        flow = outer_flow
+        started = []
+
         def store_flow(layer, row, parts):
             inverse = 1.0 / parts[0]
             at = flow_at(layer, row)
@@ -387,8 +450,6 @@
         store_flow(0, 0, both(signed([n1 + n7 + n9 + n11 + n13, n7 - n9, n11 - n13], 1), own(0, 0, NYL)))
         for place, row in enumerate(HALO_ROWS):
             store_flow(0, row, both(signed(get(left_message, 199 + 3 * place, 3, 1), 1), own(0, row, 1)))
-        for layer in range(1, NXL - 1):
-            store_flow(layer, -8, own(layer, -8, PITCH))
         n2, n8, n10, n12, n14 = get(right_message, 160, 5, NYL)
         store_flow(NXL - 1, 0, both(signed([n2 + n8 + n10 + n12 + n14, n10 - n8, n14 - n12], -1), own(NXL - 1, 0, NYL)))
         for place, row in enumerate(HALO_ROWS):
@@ -424,19 +485,19 @@
         def layer_load(layer):
             def load(axis, dx, dy):
                 at = flow_at(layer + dx, dy)
-                return flow[axis, at : at + NYL, :]
+                return flow_ref(layer + dx)[axis, at : at + NYL, :]
 
             return load
 
+        lines = lax.broadcasted_iota(jnp.int32, (NXL, NZL), 0)
+
         def row_load(axis, dx, dy):
-            return flow[axis, pl.ds(flow_at(dx, NYL + dy), NXL, stride=PITCH), :]
-
-        level = levels[index[gx * NXL // BRICK, gy * NYL // BRICK]]
-        lane = lax.broadcasted_iota(jnp.int32, (NYL, NZL), 1) // BRICK
-        shown = jnp.zeros((NYL, NZL), jnp.int32)
-        for brick in range(NZL // BRICK):
-            shown = jnp.where(lane == brick, visible[gx * NXL // BRICK, gy * NYL // BRICK, brick], shown)
-        shown = shown == 1
+            rows = pl.ds(flow_at(dx, NYL + dy), NXL, stride=PITCH)
+            inside = jnp.logical_and(lines + dx > 0, lines + dx < NXL - 1)
+            return jnp.where(inside, inner_flow[axis, rows, :], outer_flow[axis, rows, :])
+
+        shown = shades[0:1, :] > 0.5
+        level = shades[8:9, :]
 
         def crossing(here, there):
             return jnp.where(shown, jnp.maximum(-here * there, 0.0) / (here * here + there * there + 0.25), 0.0)
@@ -447,10 +508,15 @@
             scaled, following = following, scaled_at(layer_load(layer + 1))
             at = layer * NYL
             here = scaled - level
-            q_field[at : at + NYL, :] = jnp.where(shown, scaled, 0.0)
-            crossings[0, at : at + NYL, :] = crossing(here, following - level)
-            crossings[1, at : at + NYL, :] = crossing(here, shifted(scaled, above[layer : layer + 1], -1) - level)
-            crossings[2, at : at + NYL, :] = crossing(here, pltpu.roll(here, NZL - 1, 1))
+            q_held[at : at + NYL, :] = jnp.where(shown, scaled, 0.0)
+            c_held[0, at : at + NYL, :] = crossing(here, following - level)
+            c_held[1, at : at + NYL, :] = crossing(here, shifted(scaled, above[layer : layer + 1], -1) - level)
+            c_held[2, at : at + NYL, :] = crossing(here, pltpu.roll(here, NZL - 1, 1))
+            if layer % 2:
+                for copy in stores(layer - 1):
+                    copy.start()
+                    started.append(copy)
+        return started
 
     @pl.when(odd_place)
     def _():
@@ -473,44 +539,82 @@
 VMEM = pl.BlockSpec(memory_space=pltpu.VMEM)
 SMEM = pl.BlockSpec(memory_space=pltpu.SMEM)
 ANY = pl.BlockSpec(memory_space=pl.ANY)
+HBM = pl.BlockSpec(memory_space=pltpu.HBM)
 
 
 def shape(*dims):
     return jax.ShapeDtypeStruct(dims, jnp.float32)
 
 
+def held(*dims):
+    return pltpu.VMEM(dims, jnp.float32)
+
+
+LARGE = pltpu.CompilerParams(vmem_limit_bytes=61 << 20)
+SMALL = pltpu.CompilerParams(vmem_limit_bytes=8 << 20)
+
+
+def near(value):
+    return pltpu.with_memory_space_constraint(value, pltpu.VMEM)
+
+
 def per_device(populations, solid, visible, omega, iso_levels, iso_index):
     cells = NXL * NYL
-    passed, to_even, to_odd = pl.pallas_call(
+    padded = (3, (NXL + 5) * PITCH, NZL)
+    passed, to_odd, to_even = pl.pallas_call(
         collide_kernel,
-        out_shape=(shape(19, cells, NZL), shape(Y_LEN, NZL), shape(Y_LEN, NZL)),
-        in_specs=[SMEM, VMEM, VMEM],
+        out_shape=(held(19, cells, NZL), held(Y_LEN, NZL), held(Y_LEN, NZL)),
+        in_specs=[SMEM, HBM, HBM],
         out_specs=(VMEM, VMEM, VMEM),
+        compiler_params=LARGE,
+        scratch_shapes=[
+            pltpu.VMEM((19, cells, NZL), jnp.float32),
+            pltpu.VMEM((cells, NZL), jnp.int32),
+            pltpu.SemaphoreType.DMA((2, NXL)),
+        ],
     )(omega, populations.reshape(19, cells, NZL), solid.reshape(cells, NZL))
-    odd_y = swap(to_odd, "gy", 1)
-    even_y = swap(to_even, "gy", 0)
-    moments, to_even, to_odd = pl.pallas_call(
+    passed = near(passed)
+    odd_y = near(swap(to_odd, "gy", 1))
+    even_y = near(swap(to_even, "gy", 0))
+    moments = pl.pallas_call(
         moment_kernel,
-        out_shape=(shape(4, (NXL + 2) * PITCH, NZL), shape(X_LEN, NZL), shape(X_LEN, NZL)),
-        in_specs=[VMEM, VMEM, VMEM],
+        out_shape=held(4, (NXL + 2) * PITCH, NZL),
+        in_specs=[VMEM],
+        out_specs=VMEM,
+        compiler_params=SMALL,
+    )(passed)
+    moments, to_odd, to_even = pl.pallas_call(
+        joining_kernel,
+        out_shape=(held(4, (NXL + 2) * PITCH, NZL), held(X_LEN, NZL), held(X_LEN, NZL)),
+        in_specs=[VMEM, VMEM, VMEM, VMEM],
         out_specs=(VMEM, VMEM, VMEM),
-    )(passed, even_y, odd_y)
-    odd_x = swap(to_odd, "gx", 1)
-    even_x = swap(to_even, "gx", 0)
-    new = pl.pallas_call(
+        compiler_params=SMALL,
+    )(passed, odd_y, even_y, near(moments))
+    moments = near(moments)
+    odd_x = near(swap(to_odd, "gx", 1))
+    even_x = near(swap(to_even, "gx", 0))
+    new, flow, shades = pl.pallas_call(
         passing_kernel,
-        out_shape=shape(19, cells, NZL),
-        in_specs=[VMEM, VMEM, VMEM],
-        out_specs=VMEM,
-    )(passed, even_y, odd_y)
+        out_shape=(shape(19, cells, NZL), held(*padded), held(16, NZL)),
+        in_specs=[SMEM, SMEM, SMEM, VMEM, VMEM, VMEM, VMEM],
+        out_specs=(VMEM, VMEM, VMEM),
+        compiler_params=SMALL,
+    )(visible.transpose(0, 2, 1), iso_levels, iso_index, passed, odd_y, even_y, moments)
     new, q_field, crossings = pl.pallas_call(
         result_kernel,
         out_shape=(shape(19, cells, NZL), shape(cells, NZL), shape(3, cells, NZL)),
-        in_specs=[SMEM, SMEM, SMEM, VMEM, VMEM, VMEM, ANY],
-        out_specs=(ANY, VMEM, VMEM),
-        scratch_shapes=[pltpu.VMEM((3, (NXL + 5) * PITCH, NZL), jnp.float32), pltpu.SemaphoreType.DMA((5,))],
-        input_output_aliases={6: 0},
-    )(visible, iso_levels, iso_index, moments, even_x, odd_x, new)
+        in_specs=[VMEM, VMEM, VMEM, VMEM, VMEM, ANY],
+        out_specs=(ANY, ANY, ANY),
+        compiler_params=SMALL,
+        scratch_shapes=[
+            pltpu.VMEM(padded, jnp.float32),
+            pltpu.VMEM((cells, NZL), jnp.float32),
+            pltpu.VMEM((3, cells, NZL), jnp.float32),
+            pltpu.SemaphoreType.DMA((10,)),
+            pltpu.SemaphoreType.DMA((2, NXL // 2)),
+        ],
+        input_output_aliases={5: 0},
+    )(near(shades), moments, odd_x, even_x, near(flow), new)
     return (
         new.reshape(19, NXL, NYL, NZL),
         q_field.reshape(NXL, NYL, NZL),

time: 50.8 us -> 37.3 us (0.73)
  the two profiles are of different devices: /device:TPU:24 before, /device:TPU:1 now
where the time goes in v2:
time: 37.3 us; the launch traced here: 37.1 us
  starting transfers between devices  25.4 us (68%)
  Pallas kernels  6.92 us (19%)
  waiting for transfers between devices  3.36 us (9%)
  between operations  1.39 us (4%)
    ppermute x4, starting transfers between devices, swap(): return lax.ppermute(value, axis, pairs)  25.4 us
    ppermute x4, waiting for transfers between devices, swap(): return lax.ppermute(value, axis, pairs)  3.36 us
    pallas_call x1, Pallas kernels, per_device(): pl.pallas_call(passing_kernel, out_shape=(shape(19, cells, NZL), held(*pa...  2.88 us
    pallas_call x1, Pallas kernels, per_device(): pl.pallas_call(collide_kernel, out_shape=(held(19, cells, NZL), held(Y_LE...  2.29 us
    pallas_call x1, Pallas kernels, per_device(): pl.pallas_call(result_kernel, out_shape=(shape(19, cells, NZL), shape(cel...  1.37 us
  transfers between devices with their start and end apart: 4, of which 1 were waited for; matrix products, arithmetic and copies ran while one was open for 0% of the time, Pallas kernels for 8%

profile of v2, /device:TPU:1, one launch (start us, length us, event | category | flops | bytes accessed | tf_op | source)
XLA Modules:
  0.0 37.1 jit_solution(766208945855767127)
XLA Ops:
  1.3 2.3 %shard_map.85 = (f32[19,128,128]{2,1,0:T(8,128)S(1)}, f32[160,128]{1,0:T(8,128)S(1)}, f32[160,128]{1,0:T(8,128)S(1)}) custom-call(f32[1]{0:T(128)S(6)} %copy.11.omega_ref, f32[19,128,128]{2,1,0:T(8,128)} %bitcast.7, s32[128,128]{1,0:T(8,128)} %bitcast.9), custom_call_target="tpu_custom_call" | custom-call | tf_op jit(solution)/shard_map/pallas_call | solution.py:564
  3.6 9.5 %collective-permute-start = (f32[160,128]{1,0:T(8,128)S(1)}, f32[160,128]{1,0:T(8,128)S(1)}, u32[]{:S(2)}, u32[]{:S(2)}) collective-permute-start(f32[160,128]{1,0:T(8,128)S(1)} %get-tuple-element.16), channel_id=1, source_target_pairs={{0,15},{1,2},{2,1},{3,4},{4,3},{5,6},{6,5},{7,8},{8,7},{9,10},{10,... | collective-permute-start | bytes 245768 | tf_op jit(solution)/shard_map/ppermute | solution.py:536
  13.1 1.9 %collective-permute-start.1 = (f32[160,128]{1,0:T(8,128)S(1)}, f32[160,128]{1,0:T(8,128)S(1)}, u32[]{:S(2)}, u32[]{:S(2)}) collective-permute-start(f32[160,128]{1,0:T(8,128)S(1)} %get-tuple-element.17), channel_id=1, source_target_pairs={{0,1},{1,0},{2,3},{3,2},{4,5},{5,4},{6,7},{7,6},{8,9},{9,8},{10,11... | collective-permute-start | bytes 245768 | tf_op jit(solution)/shard_map/ppermute | solution.py:536
  15.0 0.1 shard_map.86.moments_in
  15.2 0.0 copy-start
  15.2 0.0 copy-start.1
  15.2 0.0 copy-start.2
  15.2 0.0 collective-permute-done.odd_in
  15.2 3.4 %collective-permute-done.1.even_in = f32[160,128]{1,0:T(8,128)S(1)} collective-permute-done((f32[160,128]{1,0:T(8,128)S(1)}, f32[160,128]{1,0:T(8,128)S(1)}, u32[]{:S(2)}, u32[]{:S(2)}) %collective-permute-start.1) | collective-permute-done | bytes 81952 | tf_op jit(solution)/shard_map/ppermute | solution.py:536
  18.6 0.2 shard_map.87
  18.8 10.5 %collective-permute-start.2 = (f32[280,128]{1,0:T(8,128)S(1)}, f32[280,128]{1,0:T(8,128)S(1)}, u32[]{:S(2)}, u32[]{:S(2)}) collective-permute-start(f32[280,128]{1,0:T(8,128)S(1)} %get-tuple-element.20), channel_id=1, source_target_pairs={{0,496},{16,32},{32,16},{48,64},{64,48},{80,96},{96,80},{112,128},... | collective-permute-start | bytes 430088 | tf_op jit(solution)/shard_map/ppermute | solution.py:536
  29.4 3.5 %collective-permute-start.3 = (f32[280,128]{1,0:T(8,128)S(1)}, f32[280,128]{1,0:T(8,128)S(1)}, u32[]{:S(2)}, u32[]{:S(2)}) collective-permute-start(f32[280,128]{1,0:T(8,128)S(1)} %get-tuple-element.21), channel_id=1, source_target_pairs={{0,16},{16,0},{32,48},{48,32},{64,80},{80,64},{96,112},{112,96},{1... | collective-permute-start | bytes 430088 | tf_op jit(solution)/shard_map/ppermute | solution.py:536
  32.8 0.0 copy-done
  32.8 0.0 copy-done.1
  32.8 0.0 copy-done.2
  32.9 2.9 %shard_map.88 = (f32[19,128,128]{2,1,0:T(8,128)}, f32[3,416,128]{2,1,0:T(8,128)S(1)}, f32[16,128]{1,0:T(8,128)S(1)}) custom-call(s32[16,8,16]{2,1,0:T(8,128)S(1)} %bitcast.6, f32[8]{0:T(128)S(1)} %copy-done.2, s32[16,16]{1,0:T(8,128)S(1)} %copy-done.1, f32[19,128,128]{2,1,0:T(8,128)S(1)} %get-tuple-element.15.passed, ...), custom_call_target="tpu_custom_call" | custom-call | tf_op jit(solution)/shard_map/pallas_call | solution.py:596
  35.7 0.0 collective-permute-done.2.odd_in
  35.7 0.0 collective-permute-done.3.even_in
  35.7 1.4 %shard_map.89 = (f32[19,128,128]{2,1,0:T(8,128)}, f32[128,128]{1,0:T(8,128)}, f32[3,128,128]{2,1,0:T(8,128)}) custom-call(f32[16,128]{1,0:T(8,128)S(1)} %get-tuple-element.19.shades, f32[4,320,128]{2,1,0:T(8,128)S(1)} %get-tuple-element.18.moments, f32[280,128]{1,0:T(8,128)S(1)} %collective-permute-done.2.odd_in, ...), custom_call_target="tpu_custom_call", output_to_operand_aliasing={{0}: (5, {})} | custom-call | tf_op jit(solution)/shard_map/pallas_call | solution.py:603
Async XLA Ops:
  3.6 11.7 %collective-permute-start = (f32[160,128]{1,0:T(8,128)S(1)}, f32[160,128]{1,0:T(8,128)S(1)}, u32[]{:S(2)}, u32[]{:S(2)}) collective-permute-start(f32[160,128]{1,0:T(8,128)S(1)} %get-tuple-element.16), channel_id=1, source_target_pairs={{0,15},{1,2},{2,1},{3,4},{4,3},{5,6},{6,5},{7,8},{8,7},{9,10},{10,... | collective-permute-start | bytes 245768 | tf_op jit(solution)/shard_map/ppermute | solution.py:536
  13.1 5.5 %collective-permute-start.1 = (f32[160,128]{1,0:T(8,128)S(1)}, f32[160,128]{1,0:T(8,128)S(1)}, u32[]{:S(2)}, u32[]{:S(2)}) collective-permute-start(f32[160,128]{1,0:T(8,128)S(1)} %get-tuple-element.17), channel_id=1, source_target_pairs={{0,1},{1,0},{2,3},{3,2},{4,5},{5,4},{6,7},{7,6},{8,9},{9,8},{10,11... | collective-permute-start | bytes 245768 | tf_op jit(solution)/shard_map/ppermute | solution.py:536
  15.2 17.6 %copy-start = (s32[16,16,8]{1,2,0:T(8,128)S(1)}, s32[16,16,8]{1,2,0:T(8,128)}, u32[]{:S(2)}) copy-start(s32[16,16,8]{1,2,0:T(8,128)} %param.8) | copy-start | bytes 24580
  15.2 17.6 %copy-start.1 = (s32[16,16]{1,0:T(8,128)S(1)}, s32[16,16]{1,0:T(8,128)}, u32[]{:S(2)}) copy-start(s32[16,16]{1,0:T(8,128)} %index.1) | copy-start | bytes 3076
  15.2 17.6 %copy-start.2 = (f32[8]{0:T(128)S(1)}, f32[8]{0:T(128)}, u32[]{:S(2)}) copy-start(f32[8]{0:T(128)} %levels.1) | copy-start | bytes 100
  18.8 16.9 %collective-permute-start.2 = (f32[280,128]{1,0:T(8,128)S(1)}, f32[280,128]{1,0:T(8,128)S(1)}, u32[]{:S(2)}, u32[]{:S(2)}) collective-permute-start(f32[280,128]{1,0:T(8,128)S(1)} %get-tuple-element.20), channel_id=1, source_target_pairs={{0,496},{16,32},{32,16},{48,64},{64,48},{80,96},{96,80},{112,128},... | collective-permute-start | bytes 430088 | tf_op jit(solution)/shard_map/ppermute | solution.py:536
  29.4 6.4 %collective-permute-start.3 = (f32[280,128]{1,0:T(8,128)S(1)}, f32[280,128]{1,0:T(8,128)S(1)}, u32[]{:S(2)}, u32[]{:S(2)}) collective-permute-start(f32[280,128]{1,0:T(8,128)S(1)} %get-tuple-element.21), channel_id=1, source_target_pairs={{0,16},{16,0},{32,48},{48,32},{64,80},{80,64},{96,112},{112,96},{1... | collective-permute-start | bytes 430088 | tf_op jit(solution)/shard_map/ppermute | solution.py:536

commit v3 on v2

--- a/solution.py
+++ b/solution.py
@@ -54,13 +54,9 @@
     return total + value if sign == 1 else total - value
 
 
-def row_moments(passed, row):
+def row_moments(load, row):
     return tile_moments(
-        {
-            number: passed[number, pl.ds(row - cy, NXL, stride=NYL), :]
-            for number, (_, cy, _) in enumerate(LATTICE)
-            if 0 <= row - cy < NYL
-        }
+        {number: load(number, row - cy) for number, (_, cy, _) in enumerate(LATTICE) if 0 <= row - cy < NYL}
     )
 
 
@@ -96,12 +92,12 @@
     return tiles, beyond, before
 
 
-def pack_y(passed, message, numbers, border, rows):
+def pack_y(load, message, numbers, border, rows):
     for place, number in enumerate(numbers):
-        message[8 * place : 8 * place + 8, :] = passed[number, pl.ds(border, NXL, stride=NYL), :]
+        message[8 * place : 8 * place + 8, :] = load(number, border)
     edge = edge_start(rows)
     for place, row in enumerate(rows):
-        tiles, beyond, before = row_moments(passed, row)
+        tiles, beyond, before = row_moments(load, row)
         for which in range(4):
             at = Y_MOMENTS + 32 * place + 8 * which
             message[at : at + 8, :] = tiles[which]
@@ -122,64 +118,85 @@
     return total
 
 
-def collide_kernel(omega_ref, pop_in, solid_in, passed, odd_message, even_message, pop, solid, sem):
-    rate = omega_ref[0]
+def collided(own, wall, rate):
     keep = 1.0 - rate
-
-    def loads(i):
-        rows = pl.ds(pl.multiple_of(i * NYL, NYL), NYL)
-        return (
-            pltpu.make_async_copy(pop_in.at[:, rows, :], pop.at[:, rows, :], sem.at[0, i]),
-            pltpu.make_async_copy(solid_in.at[rows, :], solid.at[rows, :], sem.at[1, i]),
-        )
-
+    differ = {number: own[number] - own[number + 1] for number, _ in PAIRS}
+    density = own[0]
+    for number, _ in PAIRS:
+        density = density + (own[number] + own[number + 1])
+    momentum = [combine([differ[number] for number, _ in PAIRS], [d[axis] for _, d in PAIRS]) for axis in range(3)]
+    inverse = 1.0 / density
+    velocity = [part * inverse for part in momentum]
+    base = 1.0 - 1.5 * (velocity[0] * velocity[0] + velocity[1] * velocity[1] + velocity[2] * velocity[2])
+    scale = rate * density
+    weight1, weight2 = scale * (1.0 / 18.0), scale * (1.0 / 36.0)
+    yield 0, jnp.where(wall, own[0], keep * own[0] + scale * (1.0 / 3.0) * base)
+    for number, direction in PAIRS:
+        along = combine(velocity, direction)
+        weight = weight1 if number < 7 else weight2
+        even = base + 4.5 * (along * along)
+        odd = 3.0 * along
+        plus = jnp.where(wall, own[number + 1], keep * own[number] + weight * (even + odd))
+        minus = jnp.where(wall, own[number], keep * own[number + 1] + weight * (even - odd))
+        if direction[2]:
+            plus = pltpu.roll(plus, direction[2] % NZL, 1)
+            minus = pltpu.roll(minus, -direction[2] % NZL, 1)
+        yield number, plus
+        yield number + 1, minus
+
+
+BORDER = (13, 14, 15, 0, 1, 2, 3)
+
+
+def border_kernel(
+    omega_in, visible_in, levels_in, index_in, pop_in, solid_in,
+    pop, solid, odd_message, even_message, shades,
+    border, omega, visible, levels, index, sem,
+):
+    brick_x, brick_y = lax.axis_index("gx") * NXL // BRICK, lax.axis_index("gy") * NYL // BRICK
+    pairs = [
+        (omega_in, omega),
+        (visible_in.at[brick_x], visible),
+        (levels_in, levels),
+        (index_in, index),
+        (solid_in, solid),
+    ]
     for i in range(NXL):
-        for copy in loads(i):
-            copy.start()
-
-    def layer(i, carry):
-        for copy in loads(i):
-            copy.wait()
-        rows = pl.ds(pl.multiple_of(i * NYL, NYL), NYL)
+        rows = slice(i * NYL, (i + 1) * NYL)
+        pairs.append((pop_in.at[:, rows, :], pop.at[:, rows, :]))
+    copies = [pltpu.make_async_copy(source, target, sem.at[place]) for place, (source, target) in enumerate(pairs)]
+    for copy in copies:
+        copy.start()
+    for copy in copies:
+        copy.wait()
+    rate = omega[0]
+    lane = lax.broadcasted_iota(jnp.int32, (8, NZL), 1) // BRICK
+    shown = jnp.zeros((8, NZL), jnp.int32)
+    for brick in range(NZL // BRICK):
+        shown = jnp.where(lane == brick, visible[brick, brick_y], shown)
+    shades[0:8, :] = shown.astype(jnp.float32)
+    shades[8:16, :] = jnp.full((8, NZL), levels[index[brick_x, brick_y]], jnp.float32)
+    shades[16:24, :] = jnp.full((8, NZL), rate, jnp.float32)
+    for place, row in enumerate(BORDER):
+        rows = pl.ds(row, NXL, stride=NYL)
         own = [pop[number, rows, :] for number in range(19)]
-        wall = solid[rows, :] == 1
-        differ = {number: own[number] - own[number + 1] for number, _ in PAIRS}
-        density = own[0]
-        for number, _ in PAIRS:
-            density = density + (own[number] + own[number + 1])
-        momentum = [combine([differ[number] for number, _ in PAIRS], [d[axis] for _, d in PAIRS]) for axis in range(3)]
-        inverse = 1.0 / density
-        velocity = [part * inverse for part in momentum]
-        base = 1.0 - 1.5 * (velocity[0] * velocity[0] + velocity[1] * velocity[1] + velocity[2] * velocity[2])
-        scale = rate * density
-        weight1, weight2 = scale * (1.0 / 18.0), scale * (1.0 / 36.0)
-        passed[0, rows, :] = jnp.where(wall, own[0], keep * own[0] + scale * (1.0 / 3.0) * base)
-        for number, direction in PAIRS:
-            along = combine(velocity, direction)
-            weight = weight1 if number < 7 else weight2
-            even = base + 4.5 * (along * along)
-            odd = 3.0 * along
-            plus = jnp.where(wall, own[number + 1], keep * own[number] + weight * (even + odd))
-            minus = jnp.where(wall, own[number], keep * own[number + 1] + weight * (even - odd))
-            if direction[2]:
-                plus = pltpu.roll(plus, direction[2] % NZL, 1)
-                minus = pltpu.roll(minus, -direction[2] % NZL, 1)
-            passed[number, rows, :] = plus
-            passed[number + 1, rows, :] = minus
-        return carry
-
-    lax.fori_loop(0, NXL, layer, 0)
+        for number, tile in collided(own, solid[rows, :] == 1, rate):
+            border[place, number] = tile
+
+    def load(number, row):
+        return border[BORDER.index(row), number]
+
     odd_place = lax.axis_index("gy") % 2 == 1
 
     @pl.when(odd_place)
     def _():
-        pack_y(passed, odd_message, UPWARD, NYL - 1, UP_ROWS)
-        pack_y(passed, even_message, DOWNWARD, 0, DOWN_ROWS)
+        pack_y(load, odd_message, UPWARD, NYL - 1, UP_ROWS)
+        pack_y(load, even_message, DOWNWARD, 0, DOWN_ROWS)
 
     @pl.when(jnp.logical_not(odd_place))
     def _():
-        pack_y(passed, even_message, UPWARD, NYL - 1, UP_ROWS)
-        pack_y(passed, odd_message, DOWNWARD, 0, DOWN_ROWS)
+        pack_y(load, even_message, UPWARD, NYL - 1, UP_ROWS)
+        pack_y(load, odd_message, DOWNWARD, 0, DOWN_ROWS)
 
 
 def chooser(axis, even_message, odd_message):
@@ -205,7 +222,54 @@
     return (layer + 1) * PITCH + 8 + row
 
 
-def moment_kernel(passed, moments):
+def inner_kernel(shades, pop, solid, passed, moments):
+    rate = shades[16:17, :]
+
+    def collide_layer(i, carry):
+        rows = pl.ds(pl.multiple_of(i * NYL, NYL), NYL)
+        own = [pop[number, rows, :] for number in range(19)]
+        for number, tile in collided(own, solid[rows, :] == 1, rate):
+            passed[number, rows, :] = tile
+        return carry
+
+    lax.fori_loop(0, NXL, collide_layer, 0)
+    own_moments(passed, moments)
+
+
+def flow_of(parts):
+    inverse = 1.0 / parts[0]
+    return [part * inverse for part in parts[1:]]
+
+
+def put(message, at, values):
+    for value in values:
+        message[at : at + value.shape[0], :] = value
+        at += value.shape[0]
+
+
+def whole(moments, layer):
+    at = padded_at(layer, 0)
+    return [moments[which, at : at + NYL, :] for which in range(4)]
+
+
+def pack_right_layers(moments, leaving, message):
+    last = NXL - 1
+    put(message, 0, flow_of(whole(moments, last - 1)))
+    put(message, 48, whole(moments, last))
+    put(message, 112, [leaving(number, last) for number in RIGHTWARD])
+
+
+def pack_left_layers(moments, leaving, message):
+    put(message, 0, whole(moments, 0))
+    put(message, 64, flow_of(whole(moments, 1)) + flow_of(whole(moments, 2)))
+    put(message, 160, [leaving(number, 0) for number in LEFTWARD])
+
+
+X_RIGHT, X_LEFT = 192, 240
+
+
+def own_moments(passed, moments):
+
     def source(number, layer):
         return passed[number, layer * NYL : (layer + 1) * NYL, :]
 
@@ -254,7 +318,7 @@
     dens, along_y, along_z = to_right(NXL - 1)
     store(NXL, (dens, dens, along_y, along_z))
     for row in (-1, NYL):
-        tiles, beyond, ahead = row_moments(passed, row)
+        tiles, beyond, ahead = row_moments(lambda number, at: passed[number, pl.ds(at, NXL, stride=NYL), :], row)
         store_row(moments, row, tiles, beyond, ahead)
 
 
@@ -303,21 +367,8 @@
         store_row(moments, row, tiles, beyond, ahead)
         edges[row] = (tiles, beyond, ahead)
 
-    def flow_of(parts):
-        inverse = 1.0 / parts[0]
-        return [part * inverse for part in parts[1:]]
-
-    def put(message, at, values):
-        for value in values:
-            message[at : at + value.shape[0], :] = value
-            at += value.shape[0]
-
     def line(tiles, layer):
         return [tile[layer : layer + 1] for tile in tiles]
-
-    def whole(layer):
-        at = padded_at(layer, 0)
-        return [moments[which, at : at + NYL, :] for which in range(4)]
 
     def leaving(number, layer):
         tile = passed[number, layer * NYL : (layer + 1) * NYL, :]
@@ -328,16 +379,12 @@
 
     def pack_right(message):
         last = NXL - 1
-        put(message, 0, flow_of(whole(last - 1)))
-        put(message, 48, whole(last))
-        put(message, 112, [leaving(number, last) for number in RIGHTWARD])
-        put(message, 192, flow_of(line(edges[16][0], last - 1)) + line(edges[16][0], last) + [v for row in HALO_ROWS for v in edges[row][1]])
+        pack_right_layers(moments, leaving, message)
+        put(message, X_RIGHT, flow_of(line(edges[16][0], last - 1)) + line(edges[16][0], last) + [v for row in HALO_ROWS for v in edges[row][1]])
 
     def pack_left(message):
-        put(message, 0, whole(0))
-        put(message, 64, flow_of(whole(1)) + flow_of(whole(2)))
-        put(message, 160, [leaving(number, 0) for number in LEFTWARD])
-        put(message, 240, [v for row in HALO_ROWS[:4] for v in line(edges[row][0], 0)] + flow_of(line(edges[16][0], 1)) + [v for row in HALO_ROWS for v in edges[row][2]])
+        pack_left_layers(moments, leaving, message)
+        put(message, X_LEFT, [v for row in HALO_ROWS[:4] for v in line(edges[row][0], 0)] + flow_of(line(edges[16][0], 1)) + [v for row in HALO_ROWS for v in edges[row][2]])
 
     odd_place = lax.axis_index("gx") % 2 == 1
 
@@ -352,44 +399,55 @@
         pack_right(even_out)
 
 
-def passing_kernel(visible, levels, index, passed, odd_in, even_in, moments, new, flow, shades):
+BENT = tuple(number for number in range(19) if LATTICE[number][1])
+
+
+def passing_kernel(passed, odd_in, even_in, moments, new, flow, moved, sem):
+    copies = []
+
+    def store(source, number):
+        cx = LATTICE[number][0]
+        rows = slice(max(0, cx) * NYL, (NXL + min(0, cx)) * NYL)
+        copies.append(pltpu.make_async_copy(source, new.at[number, rows, :], sem.at[number]))
+        copies[-1].start()
+
+    for number, (cx, cy, _) in enumerate(LATTICE):
+        if not cy:
+            store(passed.at[number, max(0, -cx) * NYL : (NXL - max(0, cx)) * NYL, :], number)
     before, after = chooser("gy", even_in, odd_in)
     low = {number: before(slice(8 * place, 8 * place + 8)) for place, number in enumerate(UPWARD)}
     high = {number: after(slice(8 * place, 8 * place + 8)) for place, number in enumerate(DOWNWARD)}
-    for number, (cx, cy, _) in enumerate(LATTICE):
-        for layer in range(NXL):
-            source = layer - cx
-            if not 0 <= source < NXL:
-                continue
+    for place, number in enumerate(BENT):
+        cx, cy, _ = LATTICE[number]
+        lines = (low if cy == 1 else high)[number]
+        for source in range(max(0, -cx), NXL - max(0, cx)):
             tile = passed[number, source * NYL : (source + 1) * NYL, :]
-            if cy:
-                lines = low if cy == 1 else high
-                tile = shifted(tile, lines[number][source : source + 1], cy)
-            new[number, layer * NYL : (layer + 1) * NYL, :] = tile
+            target = (source + cx) * NYL
+            moved[place, target : target + NYL, :] = shifted(tile, lines[source : source + 1], cy)
+        store(moved.at[place, max(0, cx) * NYL : (NXL + min(0, cx)) * NYL, :], number)
     for layer in range(1, NXL - 1):
         at = padded_at(layer, -8)
         inverse = 1.0 / moments[0, at : at + PITCH, :]
         to = flow_at(layer, -8)
         for axis in range(3):
             flow[axis, to : to + PITCH, :] = moments[axis + 1, at : at + PITCH, :] * inverse
-    brick_x, brick_y = lax.axis_index("gx") * NXL // BRICK, lax.axis_index("gy") * NYL // BRICK
-    lane = lax.broadcasted_iota(jnp.int32, (8, NZL), 1) // BRICK
-    shown = jnp.zeros((8, NZL), jnp.int32)
-    for brick in range(NZL // BRICK):
-        shown = jnp.where(lane == brick, visible[brick_x, brick, brick_y], shown)
-    shades[0:8, :] = shown.astype(jnp.float32)
-    shades[8:16, :] = jnp.full((8, NZL), levels[index[brick_x, brick_y]], jnp.float32)
+    for copy in copies:
+        copy.wait()
 
 
 def flow_at(layer, row):
     return (layer + 2) * PITCH + 8 + row
 
 
-def result_kernel(shades, moments, odd_in, even_in, inner_flow, new_in, new, q_field, crossings, outer_flow, q_held, c_held, sem, out_sem):
+def result_kernel(
+    shades, moments, inner_flow, odd_in, even_in, new_in,
+    new, q_field, crossings,
+    outer_flow, q_held, c_held, sem, out_sem,
+):
     del new_in
     odd_place = lax.axis_index("gx") % 2 == 1
 
-    def copies(message, start, numbers, layer, first):
+    def enters(message, start, numbers, layer, first):
         return [
             pltpu.make_async_copy(
                 message.at[start + NYL * place : start + NYL * (place + 1), :],
@@ -400,7 +458,7 @@
         ]
 
     def run(left_message, right_message):
-        copied = copies(left_message, 112, RIGHTWARD, 0, 0) + copies(right_message, 160, LEFTWARD, NXL - 1, 5)
+        copied = enters(left_message, 112, RIGHTWARD, 0, 0) + enters(right_message, 160, LEFTWARD, NXL - 1, 5)
         for copy in copied:
             copy.start()
         copied += compute(left_message, right_message)
@@ -561,50 +619,61 @@
 def per_device(populations, solid, visible, omega, iso_levels, iso_index):
     cells = NXL * NYL
     padded = (3, (NXL + 5) * PITCH, NZL)
-    passed, to_odd, to_even = pl.pallas_call(
-        collide_kernel,
-        out_shape=(held(19, cells, NZL), held(Y_LEN, NZL), held(Y_LEN, NZL)),
-        in_specs=[SMEM, HBM, HBM],
-        out_specs=(VMEM, VMEM, VMEM),
+    pop, solid, to_odd, to_even, shades = pl.pallas_call(
+        border_kernel,
+        out_shape=(
+            held(19, cells, NZL),
+            pltpu.VMEM((cells, NZL), jnp.int32),
+            held(Y_LEN, NZL),
+            held(Y_LEN, NZL),
+            held(24, NZL),
+        ),
+        in_specs=[ANY] * 6,
+        out_specs=(VMEM,) * 5,
         compiler_params=LARGE,
         scratch_shapes=[
-            pltpu.VMEM((19, cells, NZL), jnp.float32),
-            pltpu.VMEM((cells, NZL), jnp.int32),
-            pltpu.SemaphoreType.DMA((2, NXL)),
+            pltpu.VMEM((len(BORDER), 19, NXL, NZL), jnp.float32),
+            pltpu.SMEM((1,), jnp.float32),
+            pltpu.SMEM((NZL // BRICK, iso_index.shape[1]), jnp.int32),
+            pltpu.SMEM((LEVELS,), jnp.float32),
+            pltpu.SMEM(iso_index.shape, jnp.int32),
+            pltpu.SemaphoreType.DMA((NXL + 5,)),
         ],
-    )(omega, populations.reshape(19, cells, NZL), solid.reshape(cells, NZL))
-    passed = near(passed)
+    )(omega, visible.transpose(0, 2, 1), iso_levels, iso_index, populations.reshape(19, cells, NZL), solid.reshape(cells, NZL))
     odd_y = near(swap(to_odd, "gy", 1))
     even_y = near(swap(to_even, "gy", 0))
-    moments = pl.pallas_call(
-        moment_kernel,
-        out_shape=held(4, (NXL + 2) * PITCH, NZL),
-        in_specs=[VMEM],
-        out_specs=VMEM,
+    shades = near(shades)
+    passed, moments = pl.pallas_call(
+        inner_kernel,
+        out_shape=(held(19, cells, NZL), held(4, (NXL + 2) * PITCH, NZL)),
+        in_specs=[VMEM] * 3,
+        out_specs=(VMEM,) * 2,
         compiler_params=SMALL,
-    )(passed)
+    )(shades, near(pop), near(solid))
+    passed = near(passed)
     moments, to_odd, to_even = pl.pallas_call(
         joining_kernel,
         out_shape=(held(4, (NXL + 2) * PITCH, NZL), held(X_LEN, NZL), held(X_LEN, NZL)),
-        in_specs=[VMEM, VMEM, VMEM, VMEM],
-        out_specs=(VMEM, VMEM, VMEM),
+        in_specs=[VMEM] * 4,
+        out_specs=(VMEM,) * 3,
         compiler_params=SMALL,
     )(passed, odd_y, even_y, near(moments))
     moments = near(moments)
     odd_x = near(swap(to_odd, "gx", 1))
     even_x = near(swap(to_even, "gx", 0))
-    new, flow, shades = pl.pallas_call(
+    new, flow = pl.pallas_call(
         passing_kernel,
-        out_shape=(shape(19, cells, NZL), held(*padded), held(16, NZL)),
-        in_specs=[SMEM, SMEM, SMEM, VMEM, VMEM, VMEM, VMEM],
-        out_specs=(VMEM, VMEM, VMEM),
+        out_shape=(shape(19, cells, NZL), held(*padded)),
+        in_specs=[VMEM] * 4,
+        out_specs=(ANY, VMEM),
         compiler_params=SMALL,
-    )(visible.transpose(0, 2, 1), iso_levels, iso_index, passed, odd_y, even_y, moments)
+        scratch_shapes=[pltpu.VMEM((len(BENT), cells, NZL), jnp.float32), pltpu.SemaphoreType.DMA((19,))],
+    )(passed, odd_y, even_y, moments)
     new, q_field, crossings = pl.pallas_call(
         result_kernel,
         out_shape=(shape(19, cells, NZL), shape(cells, NZL), shape(3, cells, NZL)),
-        in_specs=[VMEM, VMEM, VMEM, VMEM, VMEM, ANY],
-        out_specs=(ANY, ANY, ANY),
+        in_specs=[VMEM] * 5 + [ANY],
+        out_specs=(ANY,) * 3,
         compiler_params=SMALL,
         scratch_shapes=[
             pltpu.VMEM(padded, jnp.float32),
@@ -614,7 +683,7 @@
             pltpu.SemaphoreType.DMA((2, NXL // 2)),
         ],
         input_output_aliases={5: 0},
-    )(near(shades), moments, odd_x, even_x, near(flow), new)
+    )(shades, moments, near(flow), odd_x, even_x, new)
     return (
         new.reshape(19, NXL, NYL, NZL),
         q_field.reshape(NXL, NYL, NZL),

time: 37.3 us -> 35.9 us (0.962)
  the two profiles are of different devices: /device:TPU:1 before, /device:TPU:32 now
where the time goes in v3:
time: 35.9 us; the launch traced here: 35.6 us
  starting transfers between devices  23.5 us (65%)
  Pallas kernels  5.98 us (17%)
  waiting for transfers between devices  4.74 us (13%)
  between operations  1.35 us (4%)
    ppermute x4, starting transfers between devices, swap(): return lax.ppermute(value, axis, pairs)  23.5 us
    ppermute x4, waiting for transfers between devices, swap(): return lax.ppermute(value, axis, pairs)  4.74 us
    pallas_call x1, Pallas kernels, per_device(): pl.pallas_call(border_kernel, out_shape=(held(19, cells, NZL), pltpu.VMEM...  1.99 us
    pallas_call x1, Pallas kernels, per_device(): pl.pallas_call(result_kernel, out_shape=(shape(19, cells, NZL), shape(cel...  1.36 us
    pallas_call x1, Pallas kernels, per_device(): pl.pallas_call(inner_kernel, out_shape=(held(19, cells, NZL), held(4, (NX...  1.23 us
    pallas_call x1, Pallas kernels, per_device(): pl.pallas_call(passing_kernel, out_shape=(shape(19, cells, NZL), held(*pa...  1.16 us
  transfers between devices with their start and end apart: 4, of which 2 were waited for; matrix products, arithmetic and copies ran while one was open for 0% of the time, Pallas kernels for 7%

profile of v3, /device:TPU:32, one launch (start us, length us, event | category | flops | bytes accessed | tf_op | source)
XLA Modules:
  0.0 35.6 jit_solution(12967175418267867825)
XLA Ops:
  1.3 2.0 %shard_map.85 = (f32[19,128,128]{2,1,0:T(8,128)S(1)}, s32[128,128]{1,0:T(8,128)S(1)}, f32[160,128]{1,0:T(8,128)S(1)}, f32[160,128]{1,0:T(8,128)S(1)}, f32[24,128]{1,0:T(8,128)S(1)}) custom-call(f32[1]{0:T(128)S(6)} %copy.11.omega_in, s32[16,8,16]{2,1,0:T(8,128)} %bitcast.8, f32[8]{0:T(128)} %levels_in.1, s32[16,16]{1,0:T(8,128)} %index_in.1, ...), custom_call_target="tpu_custom_call" | custom-call | tf_op jit(solution)/shard_map/pallas_call | solution.py:622
  3.3 3.8 %collective-permute-start = (f32[160,128]{1,0:T(8,128)S(1)}, f32[160,128]{1,0:T(8,128)S(1)}, u32[]{:S(2)}, u32[]{:S(2)}) collective-permute-start(f32[160,128]{1,0:T(8,128)S(1)} %get-tuple-element.22), channel_id=1, source_target_pairs={{0,15},{1,2},{2,1},{3,4},{4,3},{5,6},{6,5},{7,8},{8,7},{9,10},{10,... | collective-permute-start | bytes 245768 | tf_op jit(solution)/shard_map/ppermute | solution.py:594
  7.1 7.2 %collective-permute-start.1 = (f32[160,128]{1,0:T(8,128)S(1)}, f32[160,128]{1,0:T(8,128)S(1)}, u32[]{:S(2)}, u32[]{:S(2)}) collective-permute-start(f32[160,128]{1,0:T(8,128)S(1)} %get-tuple-element.23), channel_id=1, source_target_pairs={{0,1},{1,0},{2,3},{3,2},{4,5},{5,4},{6,7},{7,6},{8,9},{9,8},{10,11... | collective-permute-start | bytes 245768 | tf_op jit(solution)/shard_map/ppermute | solution.py:594
  14.3 1.2 %shard_map.86 = (f32[19,128,128]{2,1,0:T(8,128)S(1)}, f32[4,320,128]{2,1,0:T(8,128)S(1)}) custom-call(f32[24,128]{1,0:T(8,128)S(1)} %get-tuple-element.18.shades, f32[19,128,128]{2,1,0:T(8,128)S(1)} %get-tuple-element.19.pop, s32[128,128]{1,0:T(8,128)S(1)} %get-tuple-element.20.solid), custom_call_target="tpu_custom_call" | custom-call | tf_op jit(solution)/shard_map/pallas_call | solution.py:646
  15.5 0.0 collective-permute-done.odd_in
  15.5 1.2 %collective-permute-done.1.even_in = f32[160,128]{1,0:T(8,128)S(1)} collective-permute-done((f32[160,128]{1,0:T(8,128)S(1)}, f32[160,128]{1,0:T(8,128)S(1)}, u32[]{:S(2)}, u32[]{:S(2)}) %collective-permute-start.1) | collective-permute-done | bytes 81952 | tf_op jit(solution)/shard_map/ppermute | solution.py:594
  16.7 0.2 shard_map.87
  16.9 10.6 %collective-permute-start.2 = (f32[280,128]{1,0:T(8,128)S(1)}, f32[280,128]{1,0:T(8,128)S(1)}, u32[]{:S(2)}, u32[]{:S(2)}) collective-permute-start(f32[280,128]{1,0:T(8,128)S(1)} %get-tuple-element.27), channel_id=1, source_target_pairs={{0,496},{16,32},{32,16},{48,64},{64,48},{80,96},{96,80},{112,128},... | collective-permute-start | bytes 430088 | tf_op jit(solution)/shard_map/ppermute | solution.py:594
  27.6 1.9 %collective-permute-start.3 = (f32[280,128]{1,0:T(8,128)S(1)}, f32[280,128]{1,0:T(8,128)S(1)}, u32[]{:S(2)}, u32[]{:S(2)}) collective-permute-start(f32[280,128]{1,0:T(8,128)S(1)} %get-tuple-element.28), channel_id=1, source_target_pairs={{0,16},{16,0},{32,48},{48,32},{64,80},{80,64},{96,112},{112,96},{1... | collective-permute-start | bytes 430088 | tf_op jit(solution)/shard_map/ppermute | solution.py:594
  29.5 1.2 %shard_map.88 = (f32[19,128,128]{2,1,0:T(8,128)}, f32[3,416,128]{2,1,0:T(8,128)S(1)}) custom-call(f32[19,128,128]{2,1,0:T(8,128)S(1)} %get-tuple-element.21.passed, f32[160,128]{1,0:T(8,128)S(1)} %collective-permute-done.odd_in, f32[160,128]{1,0:T(8,128)S(1)} %collective-permute-done.1.even_in, f32[4,320,128]{2,1,0:T(8,128)S(1)} %get-tuple-element.25.moments), custom_call_target="tpu_custom_call" | custom-call | tf_op jit(solution)/shard_map/pallas_call | solution.py:664
  30.7 3.6 %collective-permute-done.2.odd_in = f32[280,128]{1,0:T(8,128)S(1)} collective-permute-done((f32[280,128]{1,0:T(8,128)S(1)}, f32[280,128]{1,0:T(8,128)S(1)}, u32[]{:S(2)}, u32[]{:S(2)}) %collective-permute-start.2) | collective-permute-done | bytes 143392 | tf_op jit(solution)/shard_map/ppermute | solution.py:594
  34.2 0.0 collective-permute-done.3.even_in
  34.2 1.4 %shard_map.89 = (f32[19,128,128]{2,1,0:T(8,128)}, f32[128,128]{1,0:T(8,128)}, f32[3,128,128]{2,1,0:T(8,128)}) custom-call(f32[24,128]{1,0:T(8,128)S(1)} %get-tuple-element.18.shades, f32[4,320,128]{2,1,0:T(8,128)S(1)} %get-tuple-element.25.moments, f32[3,416,128]{2,1,0:T(8,128)S(1)} %get-tuple-element.26.inner_flow, ...), custom_call_target="tpu_custom_call", output_to_operand_aliasing={{0}: (5, {})} | custom-call | tf_op jit(solution)/shard_map/pallas_call | solution.py:672
Async XLA Ops:
  3.3 12.3 %collective-permute-start = (f32[160,128]{1,0:T(8,128)S(1)}, f32[160,128]{1,0:T(8,128)S(1)}, u32[]{:S(2)}, u32[]{:S(2)}) collective-permute-start(f32[160,128]{1,0:T(8,128)S(1)} %get-tuple-element.22), channel_id=1, source_target_pairs={{0,15},{1,2},{2,1},{3,4},{4,3},{5,6},{6,5},{7,8},{8,7},{9,10},{10,... | collective-permute-start | bytes 245768 | tf_op jit(solution)/shard_map/ppermute | solution.py:594
  7.1 9.6 %collective-permute-start.1 = (f32[160,128]{1,0:T(8,128)S(1)}, f32[160,128]{1,0:T(8,128)S(1)}, u32[]{:S(2)}, u32[]{:S(2)}) collective-permute-start(f32[160,128]{1,0:T(8,128)S(1)} %get-tuple-element.23), channel_id=1, source_target_pairs={{0,1},{1,0},{2,3},{3,2},{4,5},{5,4},{6,7},{7,6},{8,9},{9,8},{10,11... | collective-permute-start | bytes 245768 | tf_op jit(solution)/shard_map/ppermute | solution.py:594
  16.9 17.3 %collective-permute-start.2 = (f32[280,128]{1,0:T(8,128)S(1)}, f32[280,128]{1,0:T(8,128)S(1)}, u32[]{:S(2)}, u32[]{:S(2)}) collective-permute-start(f32[280,128]{1,0:T(8,128)S(1)} %get-tuple-element.27), channel_id=1, source_target_pairs={{0,496},{16,32},{32,16},{48,64},{64,48},{80,96},{96,80},{112,128},... | collective-permute-start | bytes 430088 | tf_op jit(solution)/shard_map/ppermute | solution.py:594
  27.6 6.7 %collective-permute-start.3 = (f32[280,128]{1,0:T(8,128)S(1)}, f32[280,128]{1,0:T(8,128)S(1)}, u32[]{:S(2)}, u32[]{:S(2)}) collective-permute-start(f32[280,128]{1,0:T(8,128)S(1)} %get-tuple-element.28), channel_id=1, source_target_pairs={{0,16},{16,0},{32,48},{48,32},{64,80},{80,64},{96,112},{112,96},{1... | collective-permute-start | bytes 430088 | tf_op jit(solution)/shard_map/ppermute | solution.py:594

commit v4 on v3

--- a/solution.py
+++ b/solution.py
@@ -148,92 +148,86 @@
 BORDER = (13, 14, 15, 0, 1, 2, 3)
 
 
-def border_kernel(
-    omega_in, visible_in, levels_in, index_in, pop_in, solid_in,
-    pop, solid, odd_message, even_message, shades,
-    border, omega, visible, levels, index, sem,
+def unit_kernel(ones):
+    ones[...] = jnp.ones((8, NZL), jnp.float32)
+
+
+def border_kernel(omega, unit, pop, solid, odd_message, even_message, border):
+    rate = unit[...] * omega[0]
+    for place, row in enumerate(BORDER):
+        rows = pl.ds(row, NXL, stride=NYL)
+        own = [pop[number, rows, :] for number in range(19)]
+        for number, tile in collided(own, solid[rows, :] == 1, rate):
+            border[place, number] = tile
+
+    def load(number, row):
+        return border[BORDER.index(row), number]
+
+    odd_place = lax.axis_index("gy") % 2 == 1
+
+    @pl.when(odd_place)
+    def _():
+        pack_y(load, odd_message, UPWARD, NYL - 1, UP_ROWS)
+        pack_y(load, even_message, DOWNWARD, 0, DOWN_ROWS)
+
+    @pl.when(jnp.logical_not(odd_place))
+    def _():
+        pack_y(load, even_message, UPWARD, NYL - 1, UP_ROWS)
+        pack_y(load, odd_message, DOWNWARD, 0, DOWN_ROWS)
+
+
+def chooser(axis, even_message, odd_message):
+    odd_place = lax.axis_index(axis) % 2 == 1
+
+    def before(rows):
+        return jnp.where(odd_place, even_message[rows, :], odd_message[rows, :])
+
+    def after(rows):
+        return jnp.where(odd_place, odd_message[rows, :], even_message[rows, :])
+
+    return before, after
+
+
+def shifted(tile, fill, step):
+    row = lax.broadcasted_iota(jnp.int32, (NYL, NZL), 0)
+    if step == 1:
+        return jnp.where(row == 0, fill, pltpu.roll(tile, 1, 0))
+    return jnp.where(row == NYL - 1, fill, pltpu.roll(tile, NYL - 1, 0))
+
+
+def padded_at(layer, row):
+    return (layer + 1) * PITCH + 8 + row
+
+
+def inner_kernel(
+    omega, unit, visible_in, levels_in, index_in, pop, solid,
+    passed, moments, shades,
+    visible, levels, index, sem,
 ):
     brick_x, brick_y = lax.axis_index("gx") * NXL // BRICK, lax.axis_index("gy") * NYL // BRICK
-    pairs = [
-        (omega_in, omega),
-        (visible_in.at[brick_x], visible),
-        (levels_in, levels),
-        (index_in, index),
-        (solid_in, solid),
-    ]
-    for i in range(NXL):
-        rows = slice(i * NYL, (i + 1) * NYL)
-        pairs.append((pop_in.at[:, rows, :], pop.at[:, rows, :]))
+    pairs = ((visible_in.at[brick_x], visible), (levels_in, levels), (index_in, index))
     copies = [pltpu.make_async_copy(source, target, sem.at[place]) for place, (source, target) in enumerate(pairs)]
     for copy in copies:
         copy.start()
+    rate = unit[0:1, :] * omega[0]
+
+    def collide_layer(i, carry):
+        rows = pl.ds(pl.multiple_of(i * NYL, NYL), NYL)
+        own = [pop[number, rows, :] for number in range(19)]
+        for number, tile in collided(own, solid[rows, :] == 1, rate):
+            passed[number, rows, :] = tile
+        return carry
+
+    lax.fori_loop(0, NXL, collide_layer, 0)
+    own_moments(passed, moments)
     for copy in copies:
         copy.wait()
-    rate = omega[0]
     lane = lax.broadcasted_iota(jnp.int32, (8, NZL), 1) // BRICK
     shown = jnp.zeros((8, NZL), jnp.int32)
     for brick in range(NZL // BRICK):
         shown = jnp.where(lane == brick, visible[brick, brick_y], shown)
     shades[0:8, :] = shown.astype(jnp.float32)
     shades[8:16, :] = jnp.full((8, NZL), levels[index[brick_x, brick_y]], jnp.float32)
-    shades[16:24, :] = jnp.full((8, NZL), rate, jnp.float32)
-    for place, row in enumerate(BORDER):
-        rows = pl.ds(row, NXL, stride=NYL)
-        own = [pop[number, rows, :] for number in range(19)]
-        for number, tile in collided(own, solid[rows, :] == 1, rate):
-            border[place, number] = tile
-
-    def load(number, row):
-        return border[BORDER.index(row), number]
-
-    odd_place = lax.axis_index("gy") % 2 == 1
-
-    @pl.when(odd_place)
-    def _():
-        pack_y(load, odd_message, UPWARD, NYL - 1, UP_ROWS)
-        pack_y(load, even_message, DOWNWARD, 0, DOWN_ROWS)
-
-    @pl.when(jnp.logical_not(odd_place))
-    def _():
-        pack_y(load, even_message, UPWARD, NYL - 1, UP_ROWS)
-        pack_y(load, odd_message, DOWNWARD, 0, DOWN_ROWS)
-
-
-def chooser(axis, even_message, odd_message):
-    odd_place = lax.axis_index(axis) % 2 == 1
-
-    def before(rows):
-        return jnp.where(odd_place, even_message[rows, :], odd_message[rows, :])
-
-    def after(rows):
-        return jnp.where(odd_place, odd_message[rows, :], even_message[rows, :])
-
-    return before, after
-
-
-def shifted(tile, fill, step):
-    row = lax.broadcasted_iota(jnp.int32, (NYL, NZL), 0)
-    if step == 1:
-        return jnp.where(row == 0, fill, pltpu.roll(tile, 1, 0))
-    return jnp.where(row == NYL - 1, fill, pltpu.roll(tile, NYL - 1, 0))
-
-
-def padded_at(layer, row):
-    return (layer + 1) * PITCH + 8 + row
-
-
-def inner_kernel(shades, pop, solid, passed, moments):
-    rate = shades[16:17, :]
-
-    def collide_layer(i, carry):
-        rows = pl.ds(pl.multiple_of(i * NYL, NYL), NYL)
-        own = [pop[number, rows, :] for number in range(19)]
-        for number, tile in collided(own, solid[rows, :] == 1, rate):
-            passed[number, rows, :] = tile
-        return carry
-
-    lax.fori_loop(0, NXL, collide_layer, 0)
-    own_moments(passed, moments)
 
 
 def flow_of(parts):
@@ -608,7 +602,6 @@
     return pltpu.VMEM(dims, jnp.float32)
 
 
-LARGE = pltpu.CompilerParams(vmem_limit_bytes=61 << 20)
 SMALL = pltpu.CompilerParams(vmem_limit_bytes=8 << 20)
 
 
@@ -619,37 +612,41 @@
 def per_device(populations, solid, visible, omega, iso_levels, iso_index):
     cells = NXL * NYL
     padded = (3, (NXL + 5) * PITCH, NZL)
-    pop, solid, to_odd, to_even, shades = pl.pallas_call(
+    unit = pl.pallas_call(
+        unit_kernel,
+        out_shape=held(8, NZL),
+        in_specs=[],
+        out_specs=VMEM,
+        compiler_params=SMALL,
+        cost_estimate=pl.CostEstimate(flops=1_000_000_000, transcendentals=0, bytes_accessed=4096),
+    )()
+    unit = near(unit)
+    pop = near(populations.reshape(19, cells, NZL))
+    solid = near(solid.reshape(cells, NZL))
+    to_odd, to_even = pl.pallas_call(
         border_kernel,
-        out_shape=(
-            held(19, cells, NZL),
-            pltpu.VMEM((cells, NZL), jnp.int32),
-            held(Y_LEN, NZL),
-            held(Y_LEN, NZL),
-            held(24, NZL),
-        ),
-        in_specs=[ANY] * 6,
-        out_specs=(VMEM,) * 5,
-        compiler_params=LARGE,
+        out_shape=(held(Y_LEN, NZL), held(Y_LEN, NZL)),
+        in_specs=[SMEM, VMEM, VMEM, VMEM],
+        out_specs=(VMEM,) * 2,
+        compiler_params=SMALL,
+        scratch_shapes=[pltpu.VMEM((len(BORDER), 19, NXL, NZL), jnp.float32)],
+    )(omega, unit, pop, solid)
+    odd_y = near(swap(to_odd, "gy", 1))
+    even_y = near(swap(to_even, "gy", 0))
+    passed, moments, shades = pl.pallas_call(
+        inner_kernel,
+        out_shape=(held(19, cells, NZL), held(4, (NXL + 2) * PITCH, NZL), held(16, NZL)),
+        in_specs=[SMEM, VMEM, ANY, ANY, ANY, VMEM, VMEM],
+        out_specs=(VMEM,) * 3,
+        compiler_params=SMALL,
         scratch_shapes=[
-            pltpu.VMEM((len(BORDER), 19, NXL, NZL), jnp.float32),
-            pltpu.SMEM((1,), jnp.float32),
             pltpu.SMEM((NZL // BRICK, iso_index.shape[1]), jnp.int32),
             pltpu.SMEM((LEVELS,), jnp.float32),
             pltpu.SMEM(iso_index.shape, jnp.int32),
-            pltpu.SemaphoreType.DMA((NXL + 5,)),
+            pltpu.SemaphoreType.DMA((3,)),
         ],
-    )(omega, visible.transpose(0, 2, 1), iso_levels, iso_index, populations.reshape(19, cells, NZL), solid.reshape(cells, NZL))
-    odd_y = near(swap(to_odd, "gy", 1))
-    even_y = near(swap(to_even, "gy", 0))
+    )(omega, unit, visible.transpose(0, 2, 1), iso_levels, iso_index, pop, solid)
     shades = near(shades)
-    passed, moments = pl.pallas_call(
-        inner_kernel,
-        out_shape=(held(19, cells, NZL), held(4, (NXL + 2) * PITCH, NZL)),
-        in_specs=[VMEM] * 3,
-        out_specs=(VMEM,) * 2,
-        compiler_params=SMALL,
-    )(shades, near(pop), near(solid))
     passed = near(passed)
     moments, to_odd, to_even = pl.pallas_call(
         joining_kernel,

time: 35.9 us -> 35 us (0.975)
  Pallas kernels: 5.98 us -> 4.57 us
  local copies, waits for them, and re-layouts: 0 us -> 0.56 us
    pallas_call x1 -> x2, Pallas kernels: 1.99 us -> 0.48 us  [the longest x1 0.48 us: per_device(): pl.pallas_call(border_kernel, out_shape=(held(Y_LEN, NZL), held(Y_LEN, NZ...]
    unnamed x0 -> x10, local copies, waits for them, and re-layouts: none -> 0.56 us
where the time goes in v4:
time: 35 us; the launch traced here: 34.8 us
  starting transfers between devices  23.5 us (67%)
  waiting for transfers between devices  4.61 us (13%)
  Pallas kernels  4.57 us (13%)
  between operations  1.52 us (4%)
  local copies, waits for them, and re-layouts  0.56 us (2%)
    ppermute x4, starting transfers between devices, swap(): return lax.ppermute(value, axis, pairs)  23.5 us
    ppermute x4, waiting for transfers between devices, swap(): return lax.ppermute(value, axis, pairs)  4.61 us
    pallas_call x1, Pallas kernels, per_device(): pl.pallas_call(result_kernel, out_shape=(shape(19, cells, NZL), shape(cel...  1.36 us
    pallas_call x1, Pallas kernels, per_device(): pl.pallas_call(inner_kernel, out_shape=(held(19, cells, NZL), held(4, (NX...  1.33 us
    pallas_call x1, Pallas kernels, per_device(): pl.pallas_call(passing_kernel, out_shape=(shape(19, cells, NZL), held(*pa...  1.16 us
  transfers between devices with their start and end apart: 4, of which 2 were waited for; matrix products, arithmetic and copies ran while one was open for 0% of the time, Pallas kernels for 7%

profile of v4, /device:TPU:32, one launch (start us, length us, event | category | flops | bytes accessed | tf_op | source)
XLA Modules:
  0.0 34.8 jit_solution(13387958150102849792)
XLA Ops:
  0.6 0.0 copy-start.1
  0.6 0.0 copy-start
  0.7 0.0 copy-start.2
  0.7 0.0 copy-start.3
  0.7 0.0 copy-start.4
  1.4 0.0 copy-done.1
  1.5 0.5 %copy-done = f32[19,8,16,128]{3,2,1,0:T(8,128)S(1)} copy-done((f32[19,8,16,128]{3,2,1,0:T(8,128)S(1)}, f32[19,8,16,128]{3,2,1,0:T(8,128)}, u32[]{:S(2)}) %copy-start) | copy-done | bytes 1245208
  2.0 0.5 %shard_map.87 = (f32[160,128]{1,0:T(8,128)S(1)}, f32[160,128]{1,0:T(8,128)S(1)}) custom-call(f32[1]{0:T(128)S(6)} %copy.11.omega, f32[8,128]{1,0:T(8,128)S(1)} %shard_map.85.unit, f32[19,128,128]{2,1,0:T(8,128)S(1)} %bitcast.6, s32[128,128]{1,0:T(8,128)S(1)} %bitcast.8), custom_call_target="tpu_custom_call" | custom-call | tf_op jit(solution)/shard_map/pallas_call | solution.py:626
  2.5 3.8 %collective-permute-start = (f32[160,128]{1,0:T(8,128)S(1)}, f32[160,128]{1,0:T(8,128)S(1)}, u32[]{:S(2)}, u32[]{:S(2)}) collective-permute-start(f32[160,128]{1,0:T(8,128)S(1)} %get-tuple-element.18), channel_id=1, source_target_pairs={{0,15},{1,2},{2,1},{3,4},{4,3},{5,6},{6,5},{7,8},{8,7},{9,10},{10,... | collective-permute-start | bytes 245768 | tf_op jit(solution)/shard_map/ppermute | solution.py:588
  6.3 7.2 %collective-permute-start.1 = (f32[160,128]{1,0:T(8,128)S(1)}, f32[160,128]{1,0:T(8,128)S(1)}, u32[]{:S(2)}, u32[]{:S(2)}) collective-permute-start(f32[160,128]{1,0:T(8,128)S(1)} %get-tuple-element.19), channel_id=1, source_target_pairs={{0,1},{1,0},{2,3},{3,2},{4,5},{5,4},{6,7},{7,6},{8,9},{9,8},{10,11... | collective-permute-start | bytes 245768 | tf_op jit(solution)/shard_map/ppermute | solution.py:588
  13.5 0.0 copy-done.2
  13.5 0.0 copy-done.3
  13.5 0.0 copy-done.4
  13.5 1.3 %shard_map.86 = (f32[19,128,128]{2,1,0:T(8,128)S(1)}, f32[4,320,128]{2,1,0:T(8,128)S(1)}, f32[16,128]{1,0:T(8,128)S(1)}) custom-call(f32[1]{0:T(128)S(6)} %copy.11.omega, f32[8,128]{1,0:T(8,128)S(1)} %shard_map.85.unit, s32[16,8,16]{2,1,0:T(8,128)S(1)} %bitcast.10, f32[8]{0:T(128)S(1)} %copy-done.4, s32[16,16]{1,0:T(8,128)S(1)} %copy-done.3, ...), custom_call_target="tpu_custom_call" | custom-call | tf_op jit(solution)/shard_map/pallas_call | solution.py:636
  14.9 0.0 collective-permute-done.odd_in
  14.9 1.0 %collective-permute-done.1.even_in = f32[160,128]{1,0:T(8,128)S(1)} collective-permute-done((f32[160,128]{1,0:T(8,128)S(1)}, f32[160,128]{1,0:T(8,128)S(1)}, u32[]{:S(2)}, u32[]{:S(2)}) %collective-permute-start.1) | collective-permute-done | bytes 81952 | tf_op jit(solution)/shard_map/ppermute | solution.py:588
  15.9 0.2 shard_map.88
  16.1 10.6 %collective-permute-start.2 = (f32[280,128]{1,0:T(8,128)S(1)}, f32[280,128]{1,0:T(8,128)S(1)}, u32[]{:S(2)}, u32[]{:S(2)}) collective-permute-start(f32[280,128]{1,0:T(8,128)S(1)} %get-tuple-element.23), channel_id=1, source_target_pairs={{0,496},{16,32},{32,16},{48,64},{64,48},{80,96},{96,80},{112,128},... | collective-permute-start | bytes 430088 | tf_op jit(solution)/shard_map/ppermute | solution.py:588
  26.8 1.9 %collective-permute-start.3 = (f32[280,128]{1,0:T(8,128)S(1)}, f32[280,128]{1,0:T(8,128)S(1)}, u32[]{:S(2)}, u32[]{:S(2)}) collective-permute-start(f32[280,128]{1,0:T(8,128)S(1)} %get-tuple-element.24), channel_id=1, source_target_pairs={{0,16},{16,0},{32,48},{48,32},{64,80},{80,64},{96,112},{112,96},{1... | collective-permute-start | bytes 430088 | tf_op jit(solution)/shard_map/ppermute | solution.py:588
  28.7 1.2 %shard_map.89 = (f32[19,128,128]{2,1,0:T(8,128)}, f32[3,416,128]{2,1,0:T(8,128)S(1)}) custom-call(f32[19,128,128]{2,1,0:T(8,128)S(1)} %get-tuple-element.17.passed, f32[160,128]{1,0:T(8,128)S(1)} %collective-permute-done.odd_in, f32[160,128]{1,0:T(8,128)S(1)} %collective-permute-done.1.even_in, f32[4,320,128]{2,1,0:T(8,128)S(1)} %get-tuple-element.21.moments), custom_call_target="tpu_custom_call" | custom-call | tf_op jit(solution)/shard_map/pallas_call | solution.py:661
  29.8 3.6 %collective-permute-done.2.odd_in = f32[280,128]{1,0:T(8,128)S(1)} collective-permute-done((f32[280,128]{1,0:T(8,128)S(1)}, f32[280,128]{1,0:T(8,128)S(1)}, u32[]{:S(2)}, u32[]{:S(2)}) %collective-permute-start.2) | collective-permute-done | bytes 143392 | tf_op jit(solution)/shard_map/ppermute | solution.py:588
  33.4 0.0 collective-permute-done.3.even_in
  33.4 1.4 %shard_map.90 = (f32[19,128,128]{2,1,0:T(8,128)}, f32[128,128]{1,0:T(8,128)}, f32[3,128,128]{2,1,0:T(8,128)}) custom-call(f32[16,128]{1,0:T(8,128)S(1)} %get-tuple-element.16.shades, f32[4,320,128]{2,1,0:T(8,128)S(1)} %get-tuple-element.21.moments, f32[3,416,128]{2,1,0:T(8,128)S(1)} %get-tuple-element.22.inner_flow, ...), custom_call_target="tpu_custom_call", output_to_operand_aliasing={{0}: (5, {})} | custom-call | tf_op jit(solution)/shard_map/pallas_call | solution.py:669
  (1 shorter events, 0.0 us)
Async XLA Ops:
  0.6 0.8 %copy-start.1 = (s32[8,16,128]{2,1,0:T(8,128)S(1)}, s32[8,16,128]{2,1,0:T(8,128)}, u32[]{:S(2)}) copy-start(s32[8,16,128]{2,1,0:T(8,128)} %param.7) | copy-start | bytes 196612
  0.6 1.3 %copy-start = (f32[19,8,16,128]{3,2,1,0:T(8,128)S(1)}, f32[19,8,16,128]{3,2,1,0:T(8,128)}, u32[]{:S(2)}) copy-start(f32[19,8,16,128]{3,2,1,0:T(8,128)} %param.6) | copy-start | bytes 3735556
  0.7 12.8 %copy-start.2 = (s32[16,16,8]{1,2,0:T(8,128)S(1)}, s32[16,16,8]{1,2,0:T(8,128)}, u32[]{:S(2)}) copy-start(s32[16,16,8]{1,2,0:T(8,128)} %param.8) | copy-start | bytes 24580
  0.7 12.8 %copy-start.3 = (s32[16,16]{1,0:T(8,128)S(1)}, s32[16,16]{1,0:T(8,128)}, u32[]{:S(2)}) copy-start(s32[16,16]{1,0:T(8,128)} %index_in.1) | copy-start | bytes 3076
  0.7 12.8 %copy-start.4 = (f32[8]{0:T(128)S(1)}, f32[8]{0:T(128)}, u32[]{:S(2)}) copy-start(f32[8]{0:T(128)} %levels_in.1) | copy-start | bytes 100
  2.5 12.4 %collective-permute-start = (f32[160,128]{1,0:T(8,128)S(1)}, f32[160,128]{1,0:T(8,128)S(1)}, u32[]{:S(2)}, u32[]{:S(2)}) collective-permute-start(f32[160,128]{1,0:T(8,128)S(1)} %get-tuple-element.18), channel_id=1, source_target_pairs={{0,15},{1,2},{2,1},{3,4},{4,3},{5,6},{6,5},{7,8},{8,7},{9,10},{10,... | collective-permute-start | bytes 245768 | tf_op jit(solution)/shard_map/ppermute | solution.py:588
  6.3 9.6 %collective-permute-start.1 = (f32[160,128]{1,0:T(8,128)S(1)}, f32[160,128]{1,0:T(8,128)S(1)}, u32[]{:S(2)}, u32[]{:S(2)}) collective-permute-start(f32[160,128]{1,0:T(8,128)S(1)} %get-tuple-element.19), channel_id=1, source_target_pairs={{0,1},{1,0},{2,3},{3,2},{4,5},{5,4},{6,7},{7,6},{8,9},{9,8},{10,11... | collective-permute-start | bytes 245768 | tf_op jit(solution)/shard_map/ppermute | solution.py:588
  16.1 17.3 %collective-permute-start.2 = (f32[280,128]{1,0:T(8,128)S(1)}, f32[280,128]{1,0:T(8,128)S(1)}, u32[]{:S(2)}, u32[]{:S(2)}) collective-permute-start(f32[280,128]{1,0:T(8,128)S(1)} %get-tuple-element.23), channel_id=1, source_target_pairs={{0,496},{16,32},{32,16},{48,64},{64,48},{80,96},{96,80},{112,128},... | collective-permute-start | bytes 430088 | tf_op jit(solution)/shard_map/ppermute | solution.py:588
  26.8 6.7 %collective-permute-start.3 = (f32[280,128]{1,0:T(8,128)S(1)}, f32[280,128]{1,0:T(8,128)S(1)}, u32[]{:S(2)}, u32[]{:S(2)}) collective-permute-start(f32[280,128]{1,0:T(8,128)S(1)} %get-tuple-element.24), channel_id=1, source_target_pairs={{0,16},{16,0},{32,48},{48,32},{64,80},{80,64},{96,112},{112,96},{1... | collective-permute-start | bytes 430088 | tf_op jit(solution)/shard_map/ppermute | solution.py:588

commit v5 on v4

--- a/solution.py
+++ b/solution.py
@@ -396,7 +396,7 @@
 BENT = tuple(number for number in range(19) if LATTICE[number][1])
 
 
-def passing_kernel(passed, odd_in, even_in, moments, new, flow, moved, sem):
+def passing_kernel(passed, odd_in, even_in, moments, new, flow, parts, moved, sem):
     copies = []
 
     def store(source, number):
@@ -425,6 +425,22 @@
         to = flow_at(layer, -8)
         for axis in range(3):
             flow[axis, to : to + PITCH, :] = moments[axis + 1, at : at + PITCH, :] * inverse
+
+    def layer_load(layer):
+        def load(axis, dx, dy):
+            at = flow_at(layer + dx, dy)
+            return flow[axis, at : at + NYL, :]
+
+        return load
+
+    for layer in INNER:
+        part = flat_part(layer_load(layer))
+        rows = slice(layer * NYL, (layer + 1) * NYL)
+        if layer in MIDDLE:
+            parts[0, rows, :] = scaled_from(layer_load(layer), part)
+        else:
+            for which in range(3):
+                parts[which, rows, :] = part[which]
     for copy in copies:
         copy.wait()
 
@@ -433,8 +449,37 @@
     return (layer + 2) * PITCH + 8 + row
 
 
+def stencil(minus2, minus1, plus1, plus2):
+    return 8.0 * (plus1 - minus1) + (minus2 - plus2)
+
+
+def slopes(load, axis, second):
+    if second == 0:
+        return stencil(*[load(axis, d, 0) for d in (-2, -1, 1, 2)])
+    if second == 1:
+        return stencil(*[load(axis, 0, d) for d in (-2, -1, 1, 2)])
+    centre = load(axis, 0, 0)
+    return stencil(*[pltpu.roll(centre, -d % NZL, 1) for d in (-2, -1, 1, 2)])
+
+
+def flat_part(load):
+    g11, g22 = slopes(load, 1, 1), slopes(load, 2, 2)
+    inner = g11 * g11 + g22 * g22 + 2.0 * (slopes(load, 1, 2) * slopes(load, 2, 1))
+    return inner, slopes(load, 0, 1), slopes(load, 0, 2)
+
+
+def scaled_from(load, part):
+    inner, g01, g02 = part
+    g00, g10, g20 = (slopes(load, axis, 0) for axis in range(3))
+    return (g00 * g00 + inner + 2.0 * (g01 * g10 + g02 * g20)) * (-50.0 / 144.0)
+
+
+INNER = range(1, NXL - 1)
+MIDDLE = range(3, NXL - 3)
+
+
 def result_kernel(
-    shades, moments, inner_flow, odd_in, even_in, new_in,
+    shades, moments, inner_flow, parts, odd_in, even_in, new_in,
     new, q_field, crossings,
     outer_flow, q_held, c_held, sem, out_sem,
 ):
@@ -516,24 +561,6 @@
         for axis, value in enumerate(get(right_message, 112, 3, NYL)):
             flow[axis, flow_at(NXL + 2, 0) : flow_at(NXL + 2, NYL), :] = value
 
-        def stencil(minus2, minus1, plus1, plus2):
-            return 8.0 * (plus1 - minus1) + (minus2 - plus2)
-
-        def scaled_at(load):
-            grads = []
-            for axis in range(3):
-                centre = load(axis, 0, 0)
-                grads.append(
-                    (
-                        stencil(*[load(axis, d, 0) for d in (-2, -1, 1, 2)]),
-                        stencil(*[load(axis, 0, d) for d in (-2, -1, 1, 2)]),
-                        stencil(*[pltpu.roll(centre, -d % NZL, 1) for d in (-2, -1, 1, 2)]),
-                    )
-                )
-            inner = grads[0][0] * grads[0][0] + grads[1][1] * grads[1][1] + grads[2][2] * grads[2][2]
-            inner = inner + 2.0 * (grads[0][1] * grads[1][0] + grads[0][2] * grads[2][0] + grads[1][2] * grads[2][1])
-            return inner * (-50.0 / 144.0)
-
         def layer_load(layer):
             def load(axis, dx, dy):
                 at = flow_at(layer + dx, dy)
@@ -554,10 +581,19 @@
         def crossing(here, there):
             return jnp.where(shown, jnp.maximum(-here * there, 0.0) / (here * here + there * there + 0.25), 0.0)
 
-        above = scaled_at(row_load)
-        following = scaled_at(layer_load(0))
+        def scaled_at(layer):
+            load = layer_load(layer)
+            rows = slice(layer * NYL, (layer + 1) * NYL)
+            if layer in MIDDLE:
+                return parts[0, rows, :]
+            if layer in INNER:
+                return scaled_from(load, [parts[which, rows, :] for which in range(3)])
+            return scaled_from(load, flat_part(load))
+
+        above = scaled_from(row_load, flat_part(row_load))
+        following = scaled_at(0)
         for layer in range(NXL):
-            scaled, following = following, scaled_at(layer_load(layer + 1))
+            scaled, following = following, scaled_at(layer + 1)
             at = layer * NYL
             here = scaled - level
             q_held[at : at + NYL, :] = jnp.where(shown, scaled, 0.0)
@@ -591,7 +627,6 @@
 VMEM = pl.BlockSpec(memory_space=pltpu.VMEM)
 SMEM = pl.BlockSpec(memory_space=pltpu.SMEM)
 ANY = pl.BlockSpec(memory_space=pl.ANY)
-HBM = pl.BlockSpec(memory_space=pltpu.HBM)
 
 
 def shape(*dims):
@@ -658,18 +693,18 @@
     moments = near(moments)
     odd_x = near(swap(to_odd, "gx", 1))
     even_x = near(swap(to_even, "gx", 0))
-    new, flow = pl.pallas_call(
+    new, flow, parts = pl.pallas_call(
         passing_kernel,
-        out_shape=(shape(19, cells, NZL), held(*padded)),
+        out_shape=(shape(19, cells, NZL), held(*padded), held(3, cells, NZL)),
         in_specs=[VMEM] * 4,
-        out_specs=(ANY, VMEM),
+        out_specs=(ANY, VMEM, VMEM),
         compiler_params=SMALL,
         scratch_shapes=[pltpu.VMEM((len(BENT), cells, NZL), jnp.float32), pltpu.SemaphoreType.DMA((19,))],
     )(passed, odd_y, even_y, moments)
     new, q_field, crossings = pl.pallas_call(
         result_kernel,
         out_shape=(shape(19, cells, NZL), shape(cells, NZL), shape(3, cells, NZL)),
-        in_specs=[VMEM] * 5 + [ANY],
+        in_specs=[VMEM] * 6 + [ANY],
         out_specs=(ANY,) * 3,
         compiler_params=SMALL,
         scratch_shapes=[
@@ -679,8 +714,8 @@
             pltpu.SemaphoreType.DMA((10,)),
             pltpu.SemaphoreType.DMA((2, NXL // 2)),
         ],
-        input_output_aliases={5: 0},
-    )(shades, moments, near(flow), odd_x, even_x, new)
+        input_output_aliases={6: 0},
+    )(shades, moments, near(flow), near(parts), odd_x, even_x, new)
     return (
         new.reshape(19, NXL, NYL, NZL),
         q_field.reshape(NXL, NYL, NZL),

time: 35 us -> 34.9 us (level)
  no operation moved by 1% of the time
where the time goes in v5:
time: 34.9 us; the launch traced here: 34.6 us
  starting transfers between devices  23.5 us (67%)
  Pallas kernels  4.52 us (13%)
  waiting for transfers between devices  4.51 us (13%)
  between operations  1.52 us (4%)
  local copies, waits for them, and re-layouts  0.56 us (2%)
    ppermute x4, starting transfers between devices, swap(): return lax.ppermute(value, axis, pairs)  23.5 us
    ppermute x4, waiting for transfers between devices, swap(): return lax.ppermute(value, axis, pairs)  4.51 us
    pallas_call x1, Pallas kernels, per_device(): pl.pallas_call(inner_kernel, out_shape=(held(19, cells, NZL), held(4, (NX...  1.33 us
    pallas_call x1, Pallas kernels, per_device(): pl.pallas_call(passing_kernel, out_shape=(shape(19, cells, NZL), held(*pa...  1.25 us
    pallas_call x1, Pallas kernels, per_device(): pl.pallas_call(result_kernel, out_shape=(shape(19, cells, NZL), shape(cel...  1.21 us
  transfers between devices with their start and end apart: 4, of which 2 were waited for; matrix products, arithmetic and copies ran while one was open for 0% of the time, Pallas kernels for 7%

profile of v5, /device:TPU:32, one launch (start us, length us, event | category | flops | bytes accessed | tf_op | source)
XLA Modules:
  0.0 34.6 jit_solution(12298061356417657334)
XLA Ops:
  0.6 0.0 copy-start.1
  0.6 0.0 copy-start
  0.7 0.0 copy-start.2
  0.7 0.0 copy-start.3
  0.7 0.0 copy-start.4
  1.4 0.0 copy-done.1
  1.5 0.5 %copy-done = f32[19,8,16,128]{3,2,1,0:T(8,128)S(1)} copy-done((f32[19,8,16,128]{3,2,1,0:T(8,128)S(1)}, f32[19,8,16,128]{3,2,1,0:T(8,128)}, u32[]{:S(2)}) %copy-start) | copy-done | bytes 1245208
  2.0 0.5 %shard_map.87 = (f32[160,128]{1,0:T(8,128)S(1)}, f32[160,128]{1,0:T(8,128)S(1)}) custom-call(f32[1]{0:T(128)S(6)} %copy.11.omega, f32[8,128]{1,0:T(8,128)S(1)} %shard_map.85.unit, f32[19,128,128]{2,1,0:T(8,128)S(1)} %bitcast.6, s32[128,128]{1,0:T(8,128)S(1)} %bitcast.8), custom_call_target="tpu_custom_call" | custom-call | tf_op jit(solution)/shard_map/pallas_call | solution.py:661
  2.5 3.8 %collective-permute-start = (f32[160,128]{1,0:T(8,128)S(1)}, f32[160,128]{1,0:T(8,128)S(1)}, u32[]{:S(2)}, u32[]{:S(2)}) collective-permute-start(f32[160,128]{1,0:T(8,128)S(1)} %get-tuple-element.19), channel_id=1, source_target_pairs={{0,15},{1,2},{2,1},{3,4},{4,3},{5,6},{6,5},{7,8},{8,7},{9,10},{10,... | collective-permute-start | bytes 245768 | tf_op jit(solution)/shard_map/ppermute | solution.py:624
  6.3 7.2 %collective-permute-start.1 = (f32[160,128]{1,0:T(8,128)S(1)}, f32[160,128]{1,0:T(8,128)S(1)}, u32[]{:S(2)}, u32[]{:S(2)}) collective-permute-start(f32[160,128]{1,0:T(8,128)S(1)} %get-tuple-element.20), channel_id=1, source_target_pairs={{0,1},{1,0},{2,3},{3,2},{4,5},{5,4},{6,7},{7,6},{8,9},{9,8},{10,11... | collective-permute-start | bytes 245768 | tf_op jit(solution)/shard_map/ppermute | solution.py:624
  13.5 0.0 copy-done.2
  13.5 0.0 copy-done.3
  13.5 0.0 copy-done.4
  13.5 1.3 %shard_map.86 = (f32[19,128,128]{2,1,0:T(8,128)S(1)}, f32[4,320,128]{2,1,0:T(8,128)S(1)}, f32[16,128]{1,0:T(8,128)S(1)}) custom-call(f32[1]{0:T(128)S(6)} %copy.11.omega, f32[8,128]{1,0:T(8,128)S(1)} %shard_map.85.unit, s32[16,8,16]{2,1,0:T(8,128)S(1)} %bitcast.10, f32[8]{0:T(128)S(1)} %copy-done.4, s32[16,16]{1,0:T(8,128)S(1)} %copy-done.3, ...), custom_call_target="tpu_custom_call" | custom-call | tf_op jit(solution)/shard_map/pallas_call | solution.py:671
  14.9 0.0 collective-permute-done.odd_in
  14.9 1.0 %collective-permute-done.1.even_in = f32[160,128]{1,0:T(8,128)S(1)} collective-permute-done((f32[160,128]{1,0:T(8,128)S(1)}, f32[160,128]{1,0:T(8,128)S(1)}, u32[]{:S(2)}, u32[]{:S(2)}) %collective-permute-start.1) | collective-permute-done | bytes 81952 | tf_op jit(solution)/shard_map/ppermute | solution.py:624
  15.9 0.2 shard_map.88
  16.1 10.6 %collective-permute-start.2 = (f32[280,128]{1,0:T(8,128)S(1)}, f32[280,128]{1,0:T(8,128)S(1)}, u32[]{:S(2)}, u32[]{:S(2)}) collective-permute-start(f32[280,128]{1,0:T(8,128)S(1)} %get-tuple-element.25), channel_id=1, source_target_pairs={{0,496},{16,32},{32,16},{48,64},{64,48},{80,96},{96,80},{112,128},... | collective-permute-start | bytes 430088 | tf_op jit(solution)/shard_map/ppermute | solution.py:624
  26.8 1.9 %collective-permute-start.3 = (f32[280,128]{1,0:T(8,128)S(1)}, f32[280,128]{1,0:T(8,128)S(1)}, u32[]{:S(2)}, u32[]{:S(2)}) collective-permute-start(f32[280,128]{1,0:T(8,128)S(1)} %get-tuple-element.26), channel_id=1, source_target_pairs={{0,16},{16,0},{32,48},{48,32},{64,80},{80,64},{96,112},{112,96},{1... | collective-permute-start | bytes 430088 | tf_op jit(solution)/shard_map/ppermute | solution.py:624
  28.7 1.3 %shard_map.89 = (f32[19,128,128]{2,1,0:T(8,128)}, f32[3,416,128]{2,1,0:T(8,128)S(1)}, f32[3,128,128]{2,1,0:T(8,128)S(1)}) custom-call(f32[19,128,128]{2,1,0:T(8,128)S(1)} %get-tuple-element.18.passed, f32[160,128]{1,0:T(8,128)S(1)} %collective-permute-done.odd_in, f32[160,128]{1,0:T(8,128)S(1)} %collective-permute-done.1.even_in, ...), custom_call_target="tpu_custom_call" | custom-call | tf_op jit(solution)/shard_map/pallas_call | solution.py:696
  29.9 3.5 %collective-permute-done.2.odd_in = f32[280,128]{1,0:T(8,128)S(1)} collective-permute-done((f32[280,128]{1,0:T(8,128)S(1)}, f32[280,128]{1,0:T(8,128)S(1)}, u32[]{:S(2)}, u32[]{:S(2)}) %collective-permute-start.2) | collective-permute-done | bytes 143392 | tf_op jit(solution)/shard_map/ppermute | solution.py:624
  33.4 0.0 collective-permute-done.3.even_in
  33.4 1.2 %shard_map.90 = (f32[19,128,128]{2,1,0:T(8,128)}, f32[128,128]{1,0:T(8,128)}, f32[3,128,128]{2,1,0:T(8,128)}) custom-call(f32[16,128]{1,0:T(8,128)S(1)} %get-tuple-element.17.shades, f32[4,320,128]{2,1,0:T(8,128)S(1)} %get-tuple-element.22.moments, f32[3,416,128]{2,1,0:T(8,128)S(1)} %get-tuple-element.23.inner_flow, ...), custom_call_target="tpu_custom_call", output_to_operand_aliasing={{0}: (6, {})} | custom-call | tf_op jit(solution)/shard_map/pallas_call | solution.py:704
  (1 shorter events, 0.0 us)
Async XLA Ops:
  0.6 0.8 %copy-start.1 = (s32[8,16,128]{2,1,0:T(8,128)S(1)}, s32[8,16,128]{2,1,0:T(8,128)}, u32[]{:S(2)}) copy-start(s32[8,16,128]{2,1,0:T(8,128)} %param.7) | copy-start | bytes 196612
  0.6 1.3 %copy-start = (f32[19,8,16,128]{3,2,1,0:T(8,128)S(1)}, f32[19,8,16,128]{3,2,1,0:T(8,128)}, u32[]{:S(2)}) copy-start(f32[19,8,16,128]{3,2,1,0:T(8,128)} %param.6) | copy-start | bytes 3735556
  0.7 12.8 %copy-start.2 = (s32[16,16,8]{1,2,0:T(8,128)S(1)}, s32[16,16,8]{1,2,0:T(8,128)}, u32[]{:S(2)}) copy-start(s32[16,16,8]{1,2,0:T(8,128)} %param.8) | copy-start | bytes 24580
  0.7 12.8 %copy-start.3 = (s32[16,16]{1,0:T(8,128)S(1)}, s32[16,16]{1,0:T(8,128)}, u32[]{:S(2)}) copy-start(s32[16,16]{1,0:T(8,128)} %index_in.1) | copy-start | bytes 3076
  0.7 12.8 %copy-start.4 = (f32[8]{0:T(128)S(1)}, f32[8]{0:T(128)}, u32[]{:S(2)}) copy-start(f32[8]{0:T(128)} %levels_in.1) | copy-start | bytes 100
  2.5 12.4 %collective-permute-start = (f32[160,128]{1,0:T(8,128)S(1)}, f32[160,128]{1,0:T(8,128)S(1)}, u32[]{:S(2)}, u32[]{:S(2)}) collective-permute-start(f32[160,128]{1,0:T(8,128)S(1)} %get-tuple-element.19), channel_id=1, source_target_pairs={{0,15},{1,2},{2,1},{3,4},{4,3},{5,6},{6,5},{7,8},{8,7},{9,10},{10,... | collective-permute-start | bytes 245768 | tf_op jit(solution)/shard_map/ppermute | solution.py:624
  6.3 9.6 %collective-permute-start.1 = (f32[160,128]{1,0:T(8,128)S(1)}, f32[160,128]{1,0:T(8,128)S(1)}, u32[]{:S(2)}, u32[]{:S(2)}) collective-permute-start(f32[160,128]{1,0:T(8,128)S(1)} %get-tuple-element.20), channel_id=1, source_target_pairs={{0,1},{1,0},{2,3},{3,2},{4,5},{5,4},{6,7},{7,6},{8,9},{9,8},{10,11... | collective-permute-start | bytes 245768 | tf_op jit(solution)/shard_map/ppermute | solution.py:624
  16.1 17.3 %collective-permute-start.2 = (f32[280,128]{1,0:T(8,128)S(1)}, f32[280,128]{1,0:T(8,128)S(1)}, u32[]{:S(2)}, u32[]{:S(2)}) collective-permute-start(f32[280,128]{1,0:T(8,128)S(1)} %get-tuple-element.25), channel_id=1, source_target_pairs={{0,496},{16,32},{32,16},{48,64},{64,48},{80,96},{96,80},{112,128},... | collective-permute-start | bytes 430088 | tf_op jit(solution)/shard_map/ppermute | solution.py:624
  26.8 6.7 %collective-permute-start.3 = (f32[280,128]{1,0:T(8,128)S(1)}, f32[280,128]{1,0:T(8,128)S(1)}, u32[]{:S(2)}, u32[]{:S(2)}) collective-permute-start(f32[280,128]{1,0:T(8,128)S(1)} %get-tuple-element.26), channel_id=1, source_target_pairs={{0,16},{16,0},{32,48},{48,32},{64,80},{80,64},{96,112},{112,96},{1... | collective-permute-start | bytes 430088 | tf_op jit(solution)/shard_map/ppermute | solution.py:624

commit v6 on v5

--- a/solution.py
+++ b/solution.py
@@ -152,13 +152,20 @@
     ones[...] = jnp.ones((8, NZL), jnp.float32)
 
 
+def needed(number, row):
+    if (row == NYL - 1 and number in UPWARD) or (row == 0 and number in DOWNWARD):
+        return True
+    return row + LATTICE[number][1] in (UP_ROWS if row > NYL // 2 else DOWN_ROWS)
+
+
 def border_kernel(omega, unit, pop, solid, odd_message, even_message, border):
     rate = unit[...] * omega[0]
     for place, row in enumerate(BORDER):
         rows = pl.ds(row, NXL, stride=NYL)
         own = [pop[number, rows, :] for number in range(19)]
         for number, tile in collided(own, solid[rows, :] == 1, rate):
-            border[place, number] = tile
+            if needed(number, row):
+                border[place, number] = tile
 
     def load(number, row):
         return border[BORDER.index(row), number]
@@ -335,7 +342,9 @@
 
 
 def joining_kernel(passed, odd_in, even_in, moments_in, moments, odd_out, even_out):
-    moments[...] = moments_in[...]
+    for layer in range(-1, NXL + 1):
+        at = padded_at(layer, 0)
+        moments[:, at : at + NYL, :] = moments_in[:, at : at + NYL, :]
     before, after = chooser("gy", even_in, odd_in)
     low = {number: before(slice(8 * place, 8 * place + 8)) for place, number in enumerate(UPWARD)}
     high = {number: after(slice(8 * place, 8 * place + 8)) for place, number in enumerate(DOWNWARD)}
@@ -357,7 +366,7 @@
         beyond = [line_of(reader, at + which) for which in range(3)]
         ahead = [line_of(reader, at + 3 + which) for which in range(3)]
         if row in (-1, 16):
-            tiles, beyond, ahead = sums(load_row(moments, row), (tiles, beyond, ahead))
+            tiles, beyond, ahead = sums(load_row(moments_in, row), (tiles, beyond, ahead))
         store_row(moments, row, tiles, beyond, ahead)
         edges[row] = (tiles, beyond, ahead)
 

time: 34.9 us -> 34.8 us (level)
  no operation moved by 1% of the time
where the time goes in v6:
time: 34.8 us; the launch traced here: 34.6 us
  starting transfers between devices  23.5 us (68%)
  waiting for transfers between devices  4.51 us (13%)
  Pallas kernels  4.45 us (13%)
  between operations  1.52 us (4%)
  local copies, waits for them, and re-layouts  0.56 us (2%)
    ppermute x4, starting transfers between devices, swap(): return lax.ppermute(value, axis, pairs)  23.5 us
    ppermute x4, waiting for transfers between devices, swap(): return lax.ppermute(value, axis, pairs)  4.51 us
    pallas_call x1, Pallas kernels, per_device(): pl.pallas_call(inner_kernel, out_shape=(held(19, cells, NZL), held(4, (NX...  1.33 us
    pallas_call x1, Pallas kernels, per_device(): pl.pallas_call(passing_kernel, out_shape=(shape(19, cells, NZL), held(*pa...  1.25 us
    pallas_call x1, Pallas kernels, per_device(): pl.pallas_call(result_kernel, out_shape=(shape(19, cells, NZL), shape(cel...  1.21 us
  transfers between devices with their start and end apart: 4, of which 2 were waited for; matrix products, arithmetic and copies ran while one was open for 0% of the time, Pallas kernels for 7%

profile of v6, /device:TPU:32, one launch (start us, length us, event | category | flops | bytes accessed | tf_op | source)
XLA Modules:
  0.0 34.6 jit_solution(549811659228313046)
XLA Ops:
  0.6 0.0 copy-start.1
  0.6 0.0 copy-start
  0.7 0.0 copy-start.2
  0.7 0.0 copy-start.3
  0.7 0.0 copy-start.4
  1.4 0.0 copy-done.1
  1.5 0.5 %copy-done = f32[19,8,16,128]{3,2,1,0:T(8,128)S(1)} copy-done((f32[19,8,16,128]{3,2,1,0:T(8,128)S(1)}, f32[19,8,16,128]{3,2,1,0:T(8,128)}, u32[]{:S(2)}) %copy-start) | copy-done | bytes 1245208
  2.0 0.4 %shard_map.87 = (f32[160,128]{1,0:T(8,128)S(1)}, f32[160,128]{1,0:T(8,128)S(1)}) custom-call(f32[1]{0:T(128)S(6)} %copy.11.omega, f32[8,128]{1,0:T(8,128)S(1)} %shard_map.85.unit, f32[19,128,128]{2,1,0:T(8,128)S(1)} %bitcast.6, s32[128,128]{1,0:T(8,128)S(1)} %bitcast.8), custom_call_target="tpu_custom_call" | custom-call | tf_op jit(solution)/shard_map/pallas_call | solution.py:670
  2.4 3.8 %collective-permute-start = (f32[160,128]{1,0:T(8,128)S(1)}, f32[160,128]{1,0:T(8,128)S(1)}, u32[]{:S(2)}, u32[]{:S(2)}) collective-permute-start(f32[160,128]{1,0:T(8,128)S(1)} %get-tuple-element.19), channel_id=1, source_target_pairs={{0,15},{1,2},{2,1},{3,4},{4,3},{5,6},{6,5},{7,8},{8,7},{9,10},{10,... | collective-permute-start | bytes 245768 | tf_op jit(solution)/shard_map/ppermute | solution.py:633
  6.3 7.2 %collective-permute-start.1 = (f32[160,128]{1,0:T(8,128)S(1)}, f32[160,128]{1,0:T(8,128)S(1)}, u32[]{:S(2)}, u32[]{:S(2)}) collective-permute-start(f32[160,128]{1,0:T(8,128)S(1)} %get-tuple-element.20), channel_id=1, source_target_pairs={{0,1},{1,0},{2,3},{3,2},{4,5},{5,4},{6,7},{7,6},{8,9},{9,8},{10,11... | collective-permute-start | bytes 245768 | tf_op jit(solution)/shard_map/ppermute | solution.py:633
  13.4 0.0 copy-done.2
  13.5 0.0 copy-done.3
  13.5 0.0 copy-done.4
  13.5 1.3 %shard_map.86 = (f32[19,128,128]{2,1,0:T(8,128)S(1)}, f32[4,320,128]{2,1,0:T(8,128)S(1)}, f32[16,128]{1,0:T(8,128)S(1)}) custom-call(f32[1]{0:T(128)S(6)} %copy.11.omega, f32[8,128]{1,0:T(8,128)S(1)} %shard_map.85.unit, s32[16,8,16]{2,1,0:T(8,128)S(1)} %bitcast.10, f32[8]{0:T(128)S(1)} %copy-done.4, s32[16,16]{1,0:T(8,128)S(1)} %copy-done.3, ...), custom_call_target="tpu_custom_call" | custom-call | tf_op jit(solution)/shard_map/pallas_call | solution.py:680
  14.8 0.0 collective-permute-done.odd_in
  14.8 1.0 %collective-permute-done.1.even_in = f32[160,128]{1,0:T(8,128)S(1)} collective-permute-done((f32[160,128]{1,0:T(8,128)S(1)}, f32[160,128]{1,0:T(8,128)S(1)}, u32[]{:S(2)}, u32[]{:S(2)}) %collective-permute-start.1) | collective-permute-done | bytes 81952 | tf_op jit(solution)/shard_map/ppermute | solution.py:633
  15.8 0.2 shard_map.88
  16.1 10.6 %collective-permute-start.2 = (f32[280,128]{1,0:T(8,128)S(1)}, f32[280,128]{1,0:T(8,128)S(1)}, u32[]{:S(2)}, u32[]{:S(2)}) collective-permute-start(f32[280,128]{1,0:T(8,128)S(1)} %get-tuple-element.25), channel_id=1, source_target_pairs={{0,496},{16,32},{32,16},{48,64},{64,48},{80,96},{96,80},{112,128},... | collective-permute-start | bytes 430088 | tf_op jit(solution)/shard_map/ppermute | solution.py:633
  26.7 1.9 %collective-permute-start.3 = (f32[280,128]{1,0:T(8,128)S(1)}, f32[280,128]{1,0:T(8,128)S(1)}, u32[]{:S(2)}, u32[]{:S(2)}) collective-permute-start(f32[280,128]{1,0:T(8,128)S(1)} %get-tuple-element.26), channel_id=1, source_target_pairs={{0,16},{16,0},{32,48},{48,32},{64,80},{80,64},{96,112},{112,96},{1... | collective-permute-start | bytes 430088 | tf_op jit(solution)/shard_map/ppermute | solution.py:633
  28.6 1.3 %shard_map.89 = (f32[19,128,128]{2,1,0:T(8,128)}, f32[3,416,128]{2,1,0:T(8,128)S(1)}, f32[3,128,128]{2,1,0:T(8,128)S(1)}) custom-call(f32[19,128,128]{2,1,0:T(8,128)S(1)} %get-tuple-element.18.passed, f32[160,128]{1,0:T(8,128)S(1)} %collective-permute-done.odd_in, f32[160,128]{1,0:T(8,128)S(1)} %collective-permute-done.1.even_in, ...), custom_call_target="tpu_custom_call" | custom-call | tf_op jit(solution)/shard_map/pallas_call | solution.py:705
  29.9 3.5 %collective-permute-done.2.odd_in = f32[280,128]{1,0:T(8,128)S(1)} collective-permute-done((f32[280,128]{1,0:T(8,128)S(1)}, f32[280,128]{1,0:T(8,128)S(1)}, u32[]{:S(2)}, u32[]{:S(2)}) %collective-permute-start.2) | collective-permute-done | bytes 143392 | tf_op jit(solution)/shard_map/ppermute | solution.py:633
  33.4 0.0 collective-permute-done.3.even_in
  33.4 1.2 %shard_map.90 = (f32[19,128,128]{2,1,0:T(8,128)}, f32[128,128]{1,0:T(8,128)}, f32[3,128,128]{2,1,0:T(8,128)}) custom-call(f32[16,128]{1,0:T(8,128)S(1)} %get-tuple-element.17.shades, f32[4,320,128]{2,1,0:T(8,128)S(1)} %get-tuple-element.22.moments, f32[3,416,128]{2,1,0:T(8,128)S(1)} %get-tuple-element.23.inner_flow, ...), custom_call_target="tpu_custom_call", output_to_operand_aliasing={{0}: (6, {})} | custom-call | tf_op jit(solution)/shard_map/pallas_call | solution.py:713
  (1 shorter events, 0.0 us)
Async XLA Ops:
  0.6 0.8 %copy-start.1 = (s32[8,16,128]{2,1,0:T(8,128)S(1)}, s32[8,16,128]{2,1,0:T(8,128)}, u32[]{:S(2)}) copy-start(s32[8,16,128]{2,1,0:T(8,128)} %param.7) | copy-start | bytes 196612
  0.6 1.3 %copy-start = (f32[19,8,16,128]{3,2,1,0:T(8,128)S(1)}, f32[19,8,16,128]{3,2,1,0:T(8,128)}, u32[]{:S(2)}) copy-start(f32[19,8,16,128]{3,2,1,0:T(8,128)} %param.6) | copy-start | bytes 3735556
  0.7 12.8 %copy-start.2 = (s32[16,16,8]{1,2,0:T(8,128)S(1)}, s32[16,16,8]{1,2,0:T(8,128)}, u32[]{:S(2)}) copy-start(s32[16,16,8]{1,2,0:T(8,128)} %param.8) | copy-start | bytes 24580
  0.7 12.8 %copy-start.3 = (s32[16,16]{1,0:T(8,128)S(1)}, s32[16,16]{1,0:T(8,128)}, u32[]{:S(2)}) copy-start(s32[16,16]{1,0:T(8,128)} %index_in.1) | copy-start | bytes 3076
  0.7 12.8 %copy-start.4 = (f32[8]{0:T(128)S(1)}, f32[8]{0:T(128)}, u32[]{:S(2)}) copy-start(f32[8]{0:T(128)} %levels_in.1) | copy-start | bytes 100
  2.4 12.4 %collective-permute-start = (f32[160,128]{1,0:T(8,128)S(1)}, f32[160,128]{1,0:T(8,128)S(1)}, u32[]{:S(2)}, u32[]{:S(2)}) collective-permute-start(f32[160,128]{1,0:T(8,128)S(1)} %get-tuple-element.19), channel_id=1, source_target_pairs={{0,15},{1,2},{2,1},{3,4},{4,3},{5,6},{6,5},{7,8},{8,7},{9,10},{10,... | collective-permute-start | bytes 245768 | tf_op jit(solution)/shard_map/ppermute | solution.py:633
  6.3 9.6 %collective-permute-start.1 = (f32[160,128]{1,0:T(8,128)S(1)}, f32[160,128]{1,0:T(8,128)S(1)}, u32[]{:S(2)}, u32[]{:S(2)}) collective-permute-start(f32[160,128]{1,0:T(8,128)S(1)} %get-tuple-element.20), channel_id=1, source_target_pairs={{0,1},{1,0},{2,3},{3,2},{4,5},{5,4},{6,7},{7,6},{8,9},{9,8},{10,11... | collective-permute-start | bytes 245768 | tf_op jit(solution)/shard_map/ppermute | solution.py:633
  16.1 17.3 %collective-permute-start.2 = (f32[280,128]{1,0:T(8,128)S(1)}, f32[280,128]{1,0:T(8,128)S(1)}, u32[]{:S(2)}, u32[]{:S(2)}) collective-permute-start(f32[280,128]{1,0:T(8,128)S(1)} %get-tuple-element.25), channel_id=1, source_target_pairs={{0,496},{16,32},{32,16},{48,64},{64,48},{80,96},{96,80},{112,128},... | collective-permute-start | bytes 430088 | tf_op jit(solution)/shard_map/ppermute | solution.py:633
  26.7 6.7 %collective-permute-start.3 = (f32[280,128]{1,0:T(8,128)S(1)}, f32[280,128]{1,0:T(8,128)S(1)}, u32[]{:S(2)}, u32[]{:S(2)}) collective-permute-start(f32[280,128]{1,0:T(8,128)S(1)} %get-tuple-element.26), channel_id=1, source_target_pairs={{0,16},{16,0},{32,48},{48,32},{64,80},{80,64},{96,112},{112,96},{1... | collective-permute-start | bytes 430088 | tf_op jit(solution)/shard_map/ppermute | solution.py:633
